TPU v7x, 1024 devices: a whole 4x8x16 slice. The times are simulated.
1024 devices in a mesh: lat: 16 (over y_hi, x), lon: 64 (over y_lo, z, core).
Axes of the slice: x: 4, y: 8 (y_hi: 4, y_lo: 2; y = y_hi * 2 + y_lo), z: 16, core: 2. Of those that a mesh axis runs over, the one named last changes fastest.
Arguments:
- ens_control: bfloat16 [64, 3, 4, 64, 8192], P(None, None, None, 'lat', 'lon'), may hold values from -6 to 6
- perturbations: bfloat16 [64, 3, 4, 64, 8192], P(None, None, None, 'lat', 'lon'), may hold values from -6 to 6
- zonal_control: float32 [3, 4, 64], P(None, None, 'lat'), may hold values from -6 to 6
- spread: float32 [3, 4, 64, 8192], P(None, None, 'lat', 'lon'), may hold values from 0.3 to 3
- currents: float32 [2, 4, 64, 8192], P(None, None, 'lat', 'lon'), may hold values from -0.4 to 0.4
- sea_mask: int32 [64, 8192], P('lat', 'lon'), may hold values 0 or 1
- observed: float32 [2, 3, 4, 64, 8192], P(None, None, None, 'lat', 'lon'), may hold values from -6 to 6
- loc_reach: int32 [8], replicated, may hold values from 0 to 2, as said below
Outputs:
- ens_grad: float32 [64, 3, 4, 64, 8192], P(None, None, None, 'lat', 'lon')
- zonal_grad: float32 [3, 4, 64], P(None, None, 'lat')
Inputs may be any that keep to these rules, and one draw needn't show every extreme that they name: `loc_reach`: some block has reach 2 and some block has reach 0.
All inputs are finite; a program needn't handle non-finite values. No bound on the sum of `sea_mask` on one device may be relied on, other than what follows from the above.
Results may differ from a plain program's by a relative error of at most 0.0029.
Values may be sent and summed in bfloat16 or wider, within the bound.
No kernel may reach another device: no remote copies, remote signals or barrier semaphores. Data moves between devices by JAX's collectives and lax.ppermute only.
A program may use at most 32 MiB of HBM per device.

v0:
```python
import math

import jax
import jax.numpy as jnp
from jax import lax
from jax.sharding import PartitionSpec as P

diffusion_number = 0.2


def padded(value, sides, width, wrap):
    for axis, dim in sides:
        peers, length = (lax.axis_size(axis), value.shape[dim])
        up = [(i, (i + 1) % peers) for i in range(peers if wrap else peers - 1)]
        down = [(j, i) for i, j in up]
        last = lax.slice_in_dim(value, length - width, length, axis=dim)
        leading = lax.slice_in_dim(value, 0, width, axis=dim)
        before = lax.ppermute(last, axis, up)
        after = lax.ppermute(leading, axis, down)
        value = jnp.concatenate([before, value, after], axis=dim)
    return value


def from_behind(block, axis, distance):
    devices = range(lax.axis_size(axis))
    route = [((i - distance) % len(devices), i) for i in devices]
    return lax.ppermute(block, axis, route)


def extend(field):
    widened = padded(field, (("lon", 3),), 1, True)
    return padded(widened, (("lat", 2),), 1, False)


def sides(extended):
    inner = extended[..., 1:-1, 1:-1]
    east = extended[..., 1:-1, 2:]
    west = extended[..., 1:-1, :-2]
    north = extended[..., 2:, 1:-1]
    south = extended[..., :-2, 1:-1]
    return (inner, east, west, north, south)


def tangent(field, coeffs, sea):
    east_c, west_c, north_c, south_c = coeffs
    inner, east, west, north, south = sides(extend(field))
    centre = 1.0 - 4.0 * diffusion_number
    return sea * (
        centre * field + east_c * east + west_c * west + north_c * north + south_c * south
    )


def adjoint(field, wide_coeffs, sea):
    east_w, west_w, north_w, south_w = wide_coeffs
    masked = sea * field
    widened = extend(masked)
    centre = 1.0 - 4.0 * diffusion_number
    summed = centre * masked + sides(east_w * widened)[2]
    summed = summed + sides(west_w * widened)[1]
    summed = summed + sides(north_w * widened)[4]
    summed = summed + sides(south_w * widened)[3]
    return summed


def cycle_pairs(block, reach_max):
    shifted_list = []
    for distance in range(1, reach_max + 1):
        for direction in (1, -1):
            moved = from_behind(block, "lat", direction * distance)
            shifted_list.append((distance, direction, moved))
    return shifted_list


def band_mix(own_block, shifted_list, weights):
    summed = weights[:, 0][:, None, None, None, None] * own_block.astype(jnp.float32)
    for distance, direction, piece in shifted_list:
        summed = summed + weights[:, distance][:, None, None, None, None] * piece.astype(
            jnp.float32
        )
    return summed


def local(
    ens_control, perturbations, zonal_control, spread, currents, sea_mask, observed, loc_reach
):
    reach_max = min(2, (lax.axis_size("lat") - 1) // 2)
    members = ens_control.shape[0]
    group = members // loc_reach.shape[0]
    scale = 1.0 / math.sqrt(members - 1)
    zscale = 1.0 / math.sqrt(ens_control.shape[4] * lax.axis_size("lon"))
    distance_axis = jnp.arange(reach_max + 1).astype(jnp.float32)
    limits = loc_reach.astype(jnp.float32)[:, None] + 1.0
    block_weights = jnp.maximum(0.0, 1.0 - distance_axis[None, :] / limits)
    weights = jnp.repeat(block_weights, group, axis=0)
    sea = sea_mask.astype(jnp.float32)
    wide_flow = extend(currents)
    wide_coeffs = (
        diffusion_number - 0.5 * wide_flow[0],
        diffusion_number + 0.5 * wide_flow[0],
        diffusion_number - 0.5 * wide_flow[1],
        diffusion_number + 0.5 * wide_flow[1],
    )
    coeffs = tuple((wide_term[..., 1:-1, 1:-1] for wide_term in wide_coeffs))
    control_near = cycle_pairs(ens_control, reach_max)
    mixed = band_mix(ens_control, control_near, weights)
    ens_part = jnp.sum(perturbations.astype(jnp.float32) * mixed, axis=0)
    start = ens_part * scale + spread * zonal_control[..., None] * zscale
    first = tangent(start, coeffs, sea)
    second = tangent(first, coeffs, sea)
    weighted = first - observed[0] + adjoint(second - observed[1], wide_coeffs, sea)
    sensitivity = adjoint(weighted, wide_coeffs, sea)
    own_products = lax.optimization_barrier(
        (perturbations.astype(jnp.float32) * sensitivity * scale).astype(jnp.bfloat16)
    )
    product_near = cycle_pairs(own_products, reach_max)
    ens_grad = band_mix(own_products, product_near, weights)
    zonal_part = jnp.sum(spread * sensitivity, axis=3)
    gathered = lax.all_gather(zonal_part[None], "lon", axis=0, tiled=True)
    summed = jnp.sum(gathered, axis=0)
    zonal_grad = zonal_control + summed * zscale
    return (ens_grad, zonal_grad)


def solution(mesh):
    return jax.shard_map(
        local,
        mesh=mesh,
        in_specs=(
            P(None, None, None, "lat", "lon"),
            P(None, None, None, "lat", "lon"),
            P(None, None, "lat"),
            P(None, None, "lat", "lon"),
            P(None, None, "lat", "lon"),
            P("lat", "lon"),
            P(None, None, None, "lat", "lon"),
            P(),
        ),
        out_specs=(P(None, None, None, "lat", "lon"), P(None, None, "lat")),
        check_vma=False,
    )
```

profile of v0, /device:TPU:23, one launch (start us, length us, event | category | flops | bytes accessed | tf_op | source)
XLA Modules:
  0.0 282.8 jit_solution(9200580276871237601)
XLA Ops:
  0.6 2.5 collective-permute-start.1
  3.1 7.0 %collective-permute-start = (bf16[64,3,4,4,128]{4,3,2,1,0:T(4,128)(2,1)}, bf16[64,3,4,4,128]{4,3,2,1,0:T(4,128)(2,1)S(1)}, u32[]{:S(2)}, u32[]{:S(2)}) collective-permute-start(bf16[64,3,4,4,128]{4,3,2,1,0:T(4,128)(2,1)} %param.8), channel_id=1, source_target_pairs={{960,0},{0,64},{64,128},{128,192},{192,256},{256,320},{320,384},{3... | collective-permute-start | bytes 2359304 | tf_op jit(solution)/shard_map/ppermute | solution.py:27
  10.2 1.9 collective-permute-start.3
  12.9 5.1 %collective-permute-start.4 = (f32[2,4,4,1]{3,2,1,0:T(4,128)S(1)}, f32[2,4,4,1]{3,2,1,0:T(4,128)S(1)}, u32[]{:S(2)}, u32[]{:S(2)}) collective-permute-start(f32[2,4,4,1]{3,2,1,0:T(4,128)S(1)} %get-tuple-element.34), channel_id=1, source_target_pairs={{0,1},{1,2},{2,3},{3,4},{4,5},{5,6},{6,7},{7,8},{8,9},{9,10},{10,1... | collective-permute-start | bytes 392 | tf_op jit(solution)/shard_map/ppermute | solution.py:18
  18.1 1.9 collective-permute-start.5
  20.7 8.1 %collective-permute-start.2 = (bf16[64,3,4,4,128]{4,3,2,1,0:T(4,128)(2,1)}, bf16[64,3,4,4,128]{4,3,2,1,0:T(4,128)(2,1)S(1)}, u32[]{:S(2)}, u32[]{:S(2)}) collective-permute-start(bf16[64,3,4,4,128]{4,3,2,1,0:T(4,128)(2,1)} %param.8), channel_id=1, source_target_pairs={{896,0},{960,64},{0,128},{64,192},{128,256},{192,320},{256,384},{3... | collective-permute-start | bytes 2359304 | tf_op jit(solution)/shard_map/ppermute | solution.py:27
  29.7 1.9 collective-permute-start.6
  31.9 28.8 %collective-permute-done.6 = f32[2,4,1,130]{3,2,1,0:T(1,128)S(1)} collective-permute-done((f32[2,4,1,130]{3,2,1,0:T(1,128)S(1)}, f32[2,4,1,130]{3,2,1,0:T(1,128)S(1)}, u32[]{:S(2)}, u32[]{:S(2)}) %collective-permute-start.6) | collective-permute-done | bytes 4192 | tf_op jit(solution)/shard_map/ppermute | solution.py:18
  63.3 10.1 %collective-permute-done.7 = f32[2,4,1,130]{3,2,1,0:T(1,128)S(1)} collective-permute-done((f32[2,4,1,130]{3,2,1,0:T(1,128)S(1)}, f32[2,4,1,130]{3,2,1,0:T(1,128)S(1)}, u32[]{:S(2)}, u32[]{:S(2)}) %collective-permute-start.7) | collective-permute-done | bytes 4192 | tf_op jit(solution)/shard_map/ppermute | solution.py:19
  74.4 3.5 %fusion = f32[3,4,4,128]{3,2,1,0:T(4,128)S(1)} fusion(bf16[64,3,4,4,128]{4,3,2,1,0:T(4,128)(2,1)} %param.9, bf16[64,3,4,4,128]{4,3,2,1,0:T(4,128)(2,1)S(1)} %collective-permute-done.3, bf16[64,3,4,4,128]{4,3,2,1,0:T(4,128)(2,1)S(1)} %collective-permute-done.2, bf16[64,3,4,4,128]{4,3,2,1,0:T(4,128)(2,1)S(1)} %collective-permute-done.1, ...), kind=kLoop, calls=%fused_computation.2 | loop fusion | flops 6678528 | bytes 4743936 | tf_op jit(solution)/shard_map/reduce_sum | solution.py:106
  78.0 19.8 %collective-permute-start.9 = (f32[3,4,4,1]{3,2,1,0:T(4,128)S(1)}, f32[3,4,4,1]{3,2,1,0:T(4,128)S(1)}, u32[]{:S(2)}, u32[]{:S(2)}) collective-permute-start(f32[3,4,4,1]{3,2,1,0:T(4,128)S(1)} %get-tuple-element.32), channel_id=1, source_target_pairs={{0,1},{1,2},{2,3},{3,4},{4,5},{5,6},{6,7},{7,8},{8,9},{9,10},{10,1... | collective-permute-start | bytes 584 | tf_op jit(solution)/shard_map/ppermute | solution.py:18
  97.8 1.9 collective-permute-start.8
  99.9 3.1 %collective-permute-done.8 = f32[3,4,4,1]{3,2,1,0:T(4,128)S(1)} collective-permute-done((f32[3,4,4,1]{3,2,1,0:T(4,128)S(1)}, f32[3,4,4,1]{3,2,1,0:T(4,128)S(1)}, u32[]{:S(2)}, u32[]{:S(2)}) %collective-permute-start.8) | collective-permute-done | bytes 224 | tf_op jit(solution)/shard_map/ppermute | solution.py:19
  103.1 1.9 collective-permute-start.10
  105.1 7.6 %collective-permute-start.11 = (f32[3,4,1,130]{3,2,1,0:T(1,128)S(1)}, f32[3,4,1,130]{3,2,1,0:T(1,128)S(1)}, u32[]{:S(2)}, u32[]{:S(2)}) collective-permute-start(f32[3,4,1,130]{3,2,1,0:T(1,128)S(1)} %get-tuple-element.11), channel_id=1, source_target_pairs={{0,64},{64,128},{128,192},{192,256},{256,320},{320,384},{384,448},... | collective-permute-start | bytes 18728 | tf_op jit(solution)/shard_map/ppermute | solution.py:18
  113.7 3.0 %collective-permute-start.13 = (f32[3,4,4,1]{3,2,1,0:T(4,128)S(1)}, f32[3,4,4,1]{3,2,1,0:T(4,128)S(1)}, u32[]{:S(2)}, u32[]{:S(2)}) collective-permute-start(f32[3,4,4,1]{3,2,1,0:T(4,128)S(1)} %get-tuple-element.30), channel_id=1, source_target_pairs={{0,1},{1,2},{2,3},{3,4},{4,5},{5,6},{6,7},{7,8},{8,9},{9,10},{10,1... | collective-permute-start | bytes 584 | tf_op jit(solution)/shard_map/ppermute | solution.py:18
  116.8 12.3 %collective-permute-start.12 = (f32[3,4,4,1]{3,2,1,0:T(4,128)S(1)}, f32[3,4,4,1]{3,2,1,0:T(4,128)S(1)}, u32[]{:S(2)}, u32[]{:S(2)}) collective-permute-start(f32[3,4,4,1]{3,2,1,0:T(4,128)S(1)} %get-tuple-element.31), channel_id=1, source_target_pairs={{1,0},{2,1},{3,2},{4,3},{5,4},{6,5},{7,6},{8,7},{9,8},{10,9},{11,1... | collective-permute-start | bytes 584 | tf_op jit(solution)/shard_map/ppermute | solution.py:19
  130.1 1.9 collective-permute-start.14
  132.0 8.1 %collective-permute-start.15 = (f32[3,4,1,130]{3,2,1,0:T(1,128)S(1)}, f32[3,4,1,130]{3,2,1,0:T(1,128)S(1)}, u32[]{:S(2)}, u32[]{:S(2)}) collective-permute-start(f32[3,4,1,130]{3,2,1,0:T(1,128)S(1)} %get-tuple-element.9), channel_id=1, source_target_pairs={{0,64},{64,128},{128,192},{192,256},{256,320},{320,384},{384,448},... | collective-permute-start | bytes 18728 | tf_op jit(solution)/shard_map/ppermute | solution.py:18
  143.2 7.3 %collective-permute-start.17 = (f32[3,4,4,1]{3,2,1,0:T(4,128)S(1)}, f32[3,4,4,1]{3,2,1,0:T(4,128)S(1)}, u32[]{:S(2)}, u32[]{:S(2)}) collective-permute-start(f32[3,4,4,1]{3,2,1,0:T(4,128)S(1)} %get-tuple-element.29), channel_id=1, source_target_pairs={{1,0},{2,1},{3,2},{4,3},{5,4},{6,5},{7,6},{8,7},{9,8},{10,9},{11,1... | collective-permute-start | bytes 584 | tf_op jit(solution)/shard_map/ppermute | solution.py:19
  151.4 8.1 %collective-permute-start.18 = (f32[3,4,1,130]{3,2,1,0:T(1,128)S(1)}, f32[3,4,1,130]{3,2,1,0:T(1,128)S(1)}, u32[]{:S(2)}, u32[]{:S(2)}) collective-permute-start(f32[3,4,1,130]{3,2,1,0:T(1,128)S(1)} %get-tuple-element.6), channel_id=1, source_target_pairs={{0,64},{64,128},{128,192},{192,256},{256,320},{320,384},{384,448},... | collective-permute-start | bytes 18728 | tf_op jit(solution)/shard_map/ppermute | solution.py:18
  159.6 1.9 collective-permute-start.19
  161.5 6.7 %collective-permute-done.19 = f32[3,4,1,130]{3,2,1,0:T(1,128)S(1)} collective-permute-done((f32[3,4,1,130]{3,2,1,0:T(1,128)S(1)}, f32[3,4,1,130]{3,2,1,0:T(1,128)S(1)}, u32[]{:S(2)}, u32[]{:S(2)}) %collective-permute-start.19) | collective-permute-done | bytes 6272 | tf_op jit(solution)/shard_map/ppermute | solution.py:19
  170.5 7.9 %collective-permute-start.21 = (f32[3,4,4,1]{3,2,1,0:T(4,128)S(1)}, f32[3,4,4,1]{3,2,1,0:T(4,128)S(1)}, u32[]{:S(2)}, u32[]{:S(2)}) collective-permute-start(f32[3,4,4,1]{3,2,1,0:T(4,128)S(1)} %get-tuple-element.27), channel_id=1, source_target_pairs={{1,0},{2,1},{3,2},{4,3},{5,4},{6,5},{7,6},{8,7},{9,8},{10,9},{11,1... | collective-permute-start | bytes 584 | tf_op jit(solution)/shard_map/ppermute | solution.py:19
  179.4 1.9 collective-permute-start.22
  181.3 3.4 %collective-permute-start.23 = (f32[3,4,1,130]{3,2,1,0:T(1,128)S(1)}, f32[3,4,1,130]{3,2,1,0:T(1,128)S(1)}, u32[]{:S(2)}, u32[]{:S(2)}) collective-permute-start(f32[3,4,1,130]{3,2,1,0:T(1,128)S(1)} %get-tuple-element.5), channel_id=1, source_target_pairs={{64,0},{128,64},{192,128},{256,192},{320,256},{384,320},{448,384},... | collective-permute-start | bytes 18728 | tf_op jit(solution)/shard_map/ppermute | solution.py:19
  184.7 5.4 %collective-permute-done.23 = f32[3,4,1,130]{3,2,1,0:T(1,128)S(1)} collective-permute-done((f32[3,4,1,130]{3,2,1,0:T(1,128)S(1)}, f32[3,4,1,130]{3,2,1,0:T(1,128)S(1)}, u32[]{:S(2)}, u32[]{:S(2)}) %collective-permute-start.23) | collective-permute-done | bytes 6272 | tf_op jit(solution)/shard_map/ppermute | solution.py:19
  190.8 1.9 collective-permute-start.27
  192.8 7.9 %collective-permute-start.26 = (bf16[64,3,4,4,128]{4,3,2,1,0:T(4,128)(2,1)S(1)}, bf16[64,3,4,4,128]{4,3,2,1,0:T(4,128)(2,1)S(1)}, u32[]{:S(2)}, u32[]{:S(2)}) collective-permute-start(bf16[64,3,4,4,128]{4,3,2,1,0:T(4,128)(2,1)S(1)} %fusion.2), channel_id=1, source_target_pairs={{896,0},{960,64},{0,128},{64,192},{128,256},{192,320},{256,384},{3... | collective-permute-start | bytes 2359304 | tf_op jit(solution)/shard_map/ppermute | solution.py:27
  202.6 7.6 %collective-permute-start.24 = (bf16[64,3,4,4,128]{4,3,2,1,0:T(4,128)(2,1)S(1)}, bf16[64,3,4,4,128]{4,3,2,1,0:T(4,128)(2,1)}, u32[]{:S(2)}, u32[]{:S(2)}) collective-permute-start(bf16[64,3,4,4,128]{4,3,2,1,0:T(4,128)(2,1)S(1)} %fusion.2), channel_id=1, source_target_pairs={{960,0},{0,64},{64,128},{128,192},{192,256},{256,320},{320,384},{3... | collective-permute-start | bytes 2359304 | tf_op jit(solution)/shard_map/ppermute | solution.py:27
  210.2 67.7 %all-gather = f32[192,4,4]{2,1,0:T(4,128)S(1)} all-gather(f32[3,4,4]{2,1,0:T(4,128)S(1)} %get-tuple-element.2), channel_id=2, replica_groups=mesh['lat'=16,'lon'=64] {'lon'}, dimensions={0}, use_global_device_ids=true | all-gather | bytes 12480 | tf_op jit(solution)/shard_map/all_gather | solution.py:118
  278.6 4.2 %multiply_add_fusion = f32[64,3,4,4,128]{4,3,2,1,0:T(4,128)} fusion(bf16[64,3,4,4,128]{4,3,2,1,0:T(4,128)(2,1)S(1)} %collective-permute-done.27, bf16[64,3,4,4,128]{4,3,2,1,0:T(4,128)(2,1)S(1)} %collective-permute-done.26, bf16[64,3,4,4,128]{4,3,2,1,0:T(4,128)(2,1)S(1)} %collective-permute-done.25, bf16[64,3,4,4,128]{4,3,2,1,0:T(4,128)(2,1)} %collective-permute-done.24, ...), kind=kLoop, calls=%fused_computation.5 | loop fusion | flops 5505024 | bytes 5505792 | tf_op jit(solution)/shard_map/add | solution.py:77
  (72 shorter events, 19.1 us)
Async XLA Ops:
  0.6 73.7 %collective-permute-start.1 = (bf16[64,3,4,4,128]{4,3,2,1,0:T(4,128)(2,1)}, bf16[64,3,4,4,128]{4,3,2,1,0:T(4,128)(2,1)S(1)}, u32[]{:S(2)}, u32[]{:S(2)}) collective-permute-start(bf16[64,3,4,4,128]{4,3,2,1,0:T(4,128)(2,1)} %param.8), channel_id=1, source_target_pairs={{64,0},{128,64},{192,128},{256,192},{320,256},{384,320},{448,384},... | collective-permute-start | bytes 2359304 | tf_op jit(solution)/shard_map/ppermute | solution.py:27
  3.1 71.2 %collective-permute-start = (bf16[64,3,4,4,128]{4,3,2,1,0:T(4,128)(2,1)}, bf16[64,3,4,4,128]{4,3,2,1,0:T(4,128)(2,1)S(1)}, u32[]{:S(2)}, u32[]{:S(2)}) collective-permute-start(bf16[64,3,4,4,128]{4,3,2,1,0:T(4,128)(2,1)} %param.8), channel_id=1, source_target_pairs={{960,0},{0,64},{64,128},{128,192},{192,256},{256,320},{320,384},{3... | collective-permute-start | bytes 2359304 | tf_op jit(solution)/shard_map/ppermute | solution.py:27
  10.2 64.2 %collective-permute-start.3 = (bf16[64,3,4,4,128]{4,3,2,1,0:T(4,128)(2,1)}, bf16[64,3,4,4,128]{4,3,2,1,0:T(4,128)(2,1)S(1)}, u32[]{:S(2)}, u32[]{:S(2)}) collective-permute-start(bf16[64,3,4,4,128]{4,3,2,1,0:T(4,128)(2,1)} %param.8), channel_id=1, source_target_pairs={{128,0},{192,64},{256,128},{320,192},{384,256},{448,320},{512,384}... | collective-permute-start | bytes 2359304 | tf_op jit(solution)/shard_map/ppermute | solution.py:27
  12.9 7.7 %collective-permute-start.4 = (f32[2,4,4,1]{3,2,1,0:T(4,128)S(1)}, f32[2,4,4,1]{3,2,1,0:T(4,128)S(1)}, u32[]{:S(2)}, u32[]{:S(2)}) collective-permute-start(f32[2,4,4,1]{3,2,1,0:T(4,128)S(1)} %get-tuple-element.34), channel_id=1, source_target_pairs={{0,1},{1,2},{2,3},{3,4},{4,5},{5,6},{6,7},{7,8},{8,9},{9,10},{10,1... | collective-permute-start | bytes 392 | tf_op jit(solution)/shard_map/ppermute | solution.py:18
  18.1 10.8 %collective-permute-start.5 = (f32[2,4,4,1]{3,2,1,0:T(4,128)S(1)}, f32[2,4,4,1]{3,2,1,0:T(4,128)S(1)}, u32[]{:S(2)}, u32[]{:S(2)}) collective-permute-start(f32[2,4,4,1]{3,2,1,0:T(4,128)S(1)} %get-tuple-element.35), channel_id=1, source_target_pairs={{1,0},{2,1},{3,2},{4,3},{5,4},{6,5},{7,6},{8,7},{9,8},{10,9},{11,1... | collective-permute-start | bytes 392 | tf_op jit(solution)/shard_map/ppermute | solution.py:19
  20.7 53.7 %collective-permute-start.2 = (bf16[64,3,4,4,128]{4,3,2,1,0:T(4,128)(2,1)}, bf16[64,3,4,4,128]{4,3,2,1,0:T(4,128)(2,1)S(1)}, u32[]{:S(2)}, u32[]{:S(2)}) collective-permute-start(bf16[64,3,4,4,128]{4,3,2,1,0:T(4,128)(2,1)} %param.8), channel_id=1, source_target_pairs={{896,0},{960,64},{0,128},{64,192},{128,256},{192,320},{256,384},{3... | collective-permute-start | bytes 2359304 | tf_op jit(solution)/shard_map/ppermute | solution.py:27
  29.7 30.9 %collective-permute-start.6 = (f32[2,4,1,130]{3,2,1,0:T(1,128)S(1)}, f32[2,4,1,130]{3,2,1,0:T(1,128)S(1)}, u32[]{:S(2)}, u32[]{:S(2)}) collective-permute-start(f32[2,4,1,130]{3,2,1,0:T(1,128)S(1)} %get-tuple-element.16), channel_id=1, source_target_pairs={{0,64},{64,128},{128,192},{192,256},{256,320},{320,384},{384,448},... | collective-permute-start | bytes 12488 | tf_op jit(solution)/shard_map/ppermute | solution.py:18
  60.7 12.8 %collective-permute-start.7 = (f32[2,4,1,130]{3,2,1,0:T(1,128)S(1)}, f32[2,4,1,130]{3,2,1,0:T(1,128)S(1)}, u32[]{:S(2)}, u32[]{:S(2)}) collective-permute-start(f32[2,4,1,130]{3,2,1,0:T(1,128)S(1)} %get-tuple-element.17), channel_id=1, source_target_pairs={{64,0},{128,64},{192,128},{256,192},{320,256},{384,320},{448,384},... | collective-permute-start | bytes 12488 | tf_op jit(solution)/shard_map/ppermute | solution.py:19
  62.6 130.1 %copy-start.4 = (f32[64]{0:T(128)}, f32[64]{0:T(128)S(1)}, u32[]{:S(2)}) copy-start(f32[64]{0:T(128)S(1)} %get-tuple-element.36) | copy-start | bytes 772
  62.6 130.1 %copy-start.5 = (f32[64]{0:T(128)}, f32[64]{0:T(128)S(1)}, u32[]{:S(2)}) copy-start(f32[64]{0:T(128)S(1)} %get-tuple-element.37) | copy-start | bytes 772
  62.6 130.1 %copy-start.6 = (f32[64]{0:T(128)}, f32[64]{0:T(128)S(1)}, u32[]{:S(2)}) copy-start(f32[64]{0:T(128)S(1)} %get-tuple-element.38) | copy-start | bytes 772
  77.8 112.5 %copy-start = (bf16[64,3,4,4,128]{4,3,2,1,0:T(4,128)(2,1)S(1)}, bf16[64,3,4,4,128]{4,3,2,1,0:T(4,128)(2,1)}, u32[]{:S(2)}) copy-start(bf16[64,3,4,4,128]{4,3,2,1,0:T(4,128)(2,1)} %param.9) | copy-start | bytes 2359300
  78.0 21.9 %collective-permute-start.9 = (f32[3,4,4,1]{3,2,1,0:T(4,128)S(1)}, f32[3,4,4,1]{3,2,1,0:T(4,128)S(1)}, u32[]{:S(2)}, u32[]{:S(2)}) collective-permute-start(f32[3,4,4,1]{3,2,1,0:T(4,128)S(1)} %get-tuple-element.32), channel_id=1, source_target_pairs={{0,1},{1,2},{2,3},{3,4},{4,5},{5,6},{6,7},{7,8},{8,9},{9,10},{10,1... | collective-permute-start | bytes 584 | tf_op jit(solution)/shard_map/ppermute | solution.py:18
  97.8 5.1 %collective-permute-start.8 = (f32[3,4,4,1]{3,2,1,0:T(4,128)S(1)}, f32[3,4,4,1]{3,2,1,0:T(4,128)S(1)}, u32[]{:S(2)}, u32[]{:S(2)}) collective-permute-start(f32[3,4,4,1]{3,2,1,0:T(4,128)S(1)} %get-tuple-element.33), channel_id=1, source_target_pairs={{1,0},{2,1},{3,2},{4,3},{5,4},{6,5},{7,6},{8,7},{9,8},{10,9},{11,1... | collective-permute-start | bytes 584 | tf_op jit(solution)/shard_map/ppermute | solution.py:19
  103.1 9.6 %collective-permute-start.10 = (f32[3,4,1,130]{3,2,1,0:T(1,128)S(1)}, f32[3,4,1,130]{3,2,1,0:T(1,128)S(1)}, u32[]{:S(2)}, u32[]{:S(2)}) collective-permute-start(f32[3,4,1,130]{3,2,1,0:T(1,128)S(1)} %get-tuple-element.10), channel_id=1, source_target_pairs={{64,0},{128,64},{192,128},{256,192},{320,256},{384,320},{448,384},... | collective-permute-start | bytes 18728 | tf_op jit(solution)/shard_map/ppermute | solution.py:19
  105.1 8.4 %collective-permute-start.11 = (f32[3,4,1,130]{3,2,1,0:T(1,128)S(1)}, f32[3,4,1,130]{3,2,1,0:T(1,128)S(1)}, u32[]{:S(2)}, u32[]{:S(2)}) collective-permute-start(f32[3,4,1,130]{3,2,1,0:T(1,128)S(1)} %get-tuple-element.11), channel_id=1, source_target_pairs={{0,64},{64,128},{128,192},{192,256},{256,320},{320,384},{384,448},... | collective-permute-start | bytes 18728 | tf_op jit(solution)/shard_map/ppermute | solution.py:18
  113.7 15.4 %collective-permute-start.13 = (f32[3,4,4,1]{3,2,1,0:T(4,128)S(1)}, f32[3,4,4,1]{3,2,1,0:T(4,128)S(1)}, u32[]{:S(2)}, u32[]{:S(2)}) collective-permute-start(f32[3,4,4,1]{3,2,1,0:T(4,128)S(1)} %get-tuple-element.30), channel_id=1, source_target_pairs={{0,1},{1,2},{2,3},{3,4},{4,5},{5,6},{6,7},{7,8},{8,9},{9,10},{10,1... | collective-permute-start | bytes 584 | tf_op jit(solution)/shard_map/ppermute | solution.py:18
  116.8 13.2 %collective-permute-start.12 = (f32[3,4,4,1]{3,2,1,0:T(4,128)S(1)}, f32[3,4,4,1]{3,2,1,0:T(4,128)S(1)}, u32[]{:S(2)}, u32[]{:S(2)}) collective-permute-start(f32[3,4,4,1]{3,2,1,0:T(4,128)S(1)} %get-tuple-element.31), channel_id=1, source_target_pairs={{1,0},{2,1},{3,2},{4,3},{5,4},{6,5},{7,6},{8,7},{9,8},{10,9},{11,1... | collective-permute-start | bytes 584 | tf_op jit(solution)/shard_map/ppermute | solution.py:19
  130.1 10.1 %collective-permute-start.14 = (f32[3,4,1,130]{3,2,1,0:T(1,128)S(1)}, f32[3,4,1,130]{3,2,1,0:T(1,128)S(1)}, u32[]{:S(2)}, u32[]{:S(2)}) collective-permute-start(f32[3,4,1,130]{3,2,1,0:T(1,128)S(1)} %get-tuple-element.8), channel_id=1, source_target_pairs={{64,0},{128,64},{192,128},{256,192},{320,256},{384,320},{448,384},... | collective-permute-start | bytes 18728 | tf_op jit(solution)/shard_map/ppermute | solution.py:19
  132.0 9.0 %collective-permute-start.15 = (f32[3,4,1,130]{3,2,1,0:T(1,128)S(1)}, f32[3,4,1,130]{3,2,1,0:T(1,128)S(1)}, u32[]{:S(2)}, u32[]{:S(2)}) collective-permute-start(f32[3,4,1,130]{3,2,1,0:T(1,128)S(1)} %get-tuple-element.9), channel_id=1, source_target_pairs={{0,64},{64,128},{128,192},{192,256},{256,320},{320,384},{384,448},... | collective-permute-start | bytes 18728 | tf_op jit(solution)/shard_map/ppermute | solution.py:18
  141.2 9.2 %collective-permute-start.16 = (f32[3,4,4,1]{3,2,1,0:T(4,128)S(1)}, f32[3,4,4,1]{3,2,1,0:T(4,128)S(1)}, u32[]{:S(2)}, u32[]{:S(2)}) collective-permute-start(f32[3,4,4,1]{3,2,1,0:T(4,128)S(1)} %get-tuple-element.28), channel_id=1, source_target_pairs={{0,1},{1,2},{2,3},{3,4},{4,5},{5,6},{6,7},{7,8},{8,9},{9,10},{10,1... | collective-permute-start | bytes 584 | tf_op jit(solution)/shard_map/ppermute | solution.py:18
  143.2 8.1 %collective-permute-start.17 = (f32[3,4,4,1]{3,2,1,0:T(4,128)S(1)}, f32[3,4,4,1]{3,2,1,0:T(4,128)S(1)}, u32[]{:S(2)}, u32[]{:S(2)}) collective-permute-start(f32[3,4,4,1]{3,2,1,0:T(4,128)S(1)} %get-tuple-element.29), channel_id=1, source_target_pairs={{1,0},{2,1},{3,2},{4,3},{5,4},{6,5},{7,6},{8,7},{9,8},{10,9},{11,1... | collective-permute-start | bytes 584 | tf_op jit(solution)/shard_map/ppermute | solution.py:19
  151.4 10.1 %collective-permute-start.18 = (f32[3,4,1,130]{3,2,1,0:T(1,128)S(1)}, f32[3,4,1,130]{3,2,1,0:T(1,128)S(1)}, u32[]{:S(2)}, u32[]{:S(2)}) collective-permute-start(f32[3,4,1,130]{3,2,1,0:T(1,128)S(1)} %get-tuple-element.6), channel_id=1, source_target_pairs={{0,64},{64,128},{128,192},{192,256},{256,320},{320,384},{384,448},... | collective-permute-start | bytes 18728 | tf_op jit(solution)/shard_map/ppermute | solution.py:18
  159.6 8.7 %collective-permute-start.19 = (f32[3,4,1,130]{3,2,1,0:T(1,128)S(1)}, f32[3,4,1,130]{3,2,1,0:T(1,128)S(1)}, u32[]{:S(2)}, u32[]{:S(2)}) collective-permute-start(f32[3,4,1,130]{3,2,1,0:T(1,128)S(1)} %get-tuple-element.7), channel_id=1, source_target_pairs={{64,0},{128,64},{192,128},{256,192},{320,256},{384,320},{448,384},... | collective-permute-start | bytes 18728 | tf_op jit(solution)/shard_map/ppermute | solution.py:19
  168.6 9.8 %collective-permute-start.20 = (f32[3,4,4,1]{3,2,1,0:T(4,128)S(1)}, f32[3,4,4,1]{3,2,1,0:T(4,128)S(1)}, u32[]{:S(2)}, u32[]{:S(2)}) collective-permute-start(f32[3,4,4,1]{3,2,1,0:T(4,128)S(1)} %get-tuple-element.26), channel_id=1, source_target_pairs={{0,1},{1,2},{2,3},{3,4},{4,5},{5,6},{6,7},{7,8},{8,9},{9,10},{10,1... | collective-permute-start | bytes 584 | tf_op jit(solution)/shard_map/ppermute | solution.py:18
  170.5 8.7 %collective-permute-start.21 = (f32[3,4,4,1]{3,2,1,0:T(4,128)S(1)}, f32[3,4,4,1]{3,2,1,0:T(4,128)S(1)}, u32[]{:S(2)}, u32[]{:S(2)}) collective-permute-start(f32[3,4,4,1]{3,2,1,0:T(4,128)S(1)} %get-tuple-element.27), channel_id=1, source_target_pairs={{1,0},{2,1},{3,2},{4,3},{5,4},{6,5},{7,6},{8,7},{9,8},{10,9},{11,1... | collective-permute-start | bytes 584 | tf_op jit(solution)/shard_map/ppermute | solution.py:19
  179.4 5.3 %collective-permute-start.22 = (f32[3,4,1,130]{3,2,1,0:T(1,128)S(1)}, f32[3,4,1,130]{3,2,1,0:T(1,128)S(1)}, u32[]{:S(2)}, u32[]{:S(2)}) collective-permute-start(f32[3,4,1,130]{3,2,1,0:T(1,128)S(1)} %get-tuple-element.4), channel_id=1, source_target_pairs={{0,64},{64,128},{128,192},{192,256},{256,320},{320,384},{384,448},... | collective-permute-start | bytes 18728 | tf_op jit(solution)/shard_map/ppermute | solution.py:18
  181.3 8.8 %collective-permute-start.23 = (f32[3,4,1,130]{3,2,1,0:T(1,128)S(1)}, f32[3,4,1,130]{3,2,1,0:T(1,128)S(1)}, u32[]{:S(2)}, u32[]{:S(2)}) collective-permute-start(f32[3,4,1,130]{3,2,1,0:T(1,128)S(1)} %get-tuple-element.5), channel_id=1, source_target_pairs={{64,0},{128,64},{192,128},{256,192},{320,256},{384,320},{448,384},... | collective-permute-start | bytes 18728 | tf_op jit(solution)/shard_map/ppermute | solution.py:19
  190.8 87.8 %collective-permute-start.27 = (bf16[64,3,4,4,128]{4,3,2,1,0:T(4,128)(2,1)S(1)}, bf16[64,3,4,4,128]{4,3,2,1,0:T(4,128)(2,1)S(1)}, u32[]{:S(2)}, u32[]{:S(2)}) collective-permute-start(bf16[64,3,4,4,128]{4,3,2,1,0:T(4,128)(2,1)S(1)} %fusion.2), channel_id=1, source_target_pairs={{128,0},{192,64},{256,128},{320,192},{384,256},{448,320},{512,384}... | collective-permute-start | bytes 2359304 | tf_op jit(solution)/shard_map/ppermute | solution.py:27
  192.8 85.8 %collective-permute-start.26 = (bf16[64,3,4,4,128]{4,3,2,1,0:T(4,128)(2,1)S(1)}, bf16[64,3,4,4,128]{4,3,2,1,0:T(4,128)(2,1)S(1)}, u32[]{:S(2)}, u32[]{:S(2)}) collective-permute-start(bf16[64,3,4,4,128]{4,3,2,1,0:T(4,128)(2,1)S(1)} %fusion.2), channel_id=1, source_target_pairs={{896,0},{960,64},{0,128},{64,192},{128,256},{192,320},{256,384},{3... | collective-permute-start | bytes 2359304 | tf_op jit(solution)/shard_map/ppermute | solution.py:27
  200.6 77.9 %collective-permute-start.25 = (bf16[64,3,4,4,128]{4,3,2,1,0:T(4,128)(2,1)S(1)}, bf16[64,3,4,4,128]{4,3,2,1,0:T(4,128)(2,1)S(1)}, u32[]{:S(2)}, u32[]{:S(2)}) collective-permute-start(bf16[64,3,4,4,128]{4,3,2,1,0:T(4,128)(2,1)S(1)} %fusion.2), channel_id=1, source_target_pairs={{64,0},{128,64},{192,128},{256,192},{320,256},{384,320},{448,384},... | collective-permute-start | bytes 2359304 | tf_op jit(solution)/shard_map/ppermute | solution.py:27
  202.6 76.0 %collective-permute-start.24 = (bf16[64,3,4,4,128]{4,3,2,1,0:T(4,128)(2,1)S(1)}, bf16[64,3,4,4,128]{4,3,2,1,0:T(4,128)(2,1)}, u32[]{:S(2)}, u32[]{:S(2)}) collective-permute-start(bf16[64,3,4,4,128]{4,3,2,1,0:T(4,128)(2,1)S(1)} %fusion.2), channel_id=1, source_target_pairs={{960,0},{0,64},{64,128},{128,192},{192,256},{256,320},{320,384},{3... | collective-permute-start | bytes 2359304 | tf_op jit(solution)/shard_map/ppermute | solution.py:27
  (3 other events, 73.6 us)
where the time goes:
time: 284 us; the launch traced here: 283 us
  starting transfers between devices  141 us (50%)
  blocking collectives  67.7 us (24%)
  waiting for transfers between devices  58.1 us (20%)
  other arithmetic  13.5 us (5%)
    all_gather x1, blocking collectives, local(): gathered = lax.all_gather(zonal_part[None], 'lon', axis=0, tiled=True)  67.7 us
    ppermute x10, starting transfers between devices, padded(): before = lax.ppermute(last, axis, up)  59.5 us
    ppermute x10, starting transfers between devices, padded(): after = lax.ppermute(leading, axis, down)  42.3 us
    ppermute x8, starting transfers between devices, from_behind(): return lax.ppermute(block, axis, route)  38.9 us
    ppermute x10, waiting for transfers between devices, padded(): before = lax.ppermute(last, axis, up)  30.3 us
    ppermute x10, waiting for transfers between devices, padded(): after = lax.ppermute(leading, axis, down)  27.8 us
  transfers between devices with their start and end apart: 28, of which 10 were waited for; matrix products, arithmetic and copies ran while one was open for 2% of the time, Pallas kernels for 0%

commit v1 on v0

v1 whole, which is shorter than its diff:
```python
import math

import jax
import jax.numpy as jnp
from jax import lax
from jax.sharding import PartitionSpec as P

NU = 0.2
HALO = 4


def cyc(value, axis, distance):
    peers = lax.axis_size(axis)
    return lax.ppermute(value, axis, [((i - distance) % peers, i) for i in range(peers)])


def open_step(value, axis, distance):
    peers = lax.axis_size(axis)
    route = [(i - distance, i) for i in range(peers) if 0 <= i - distance < peers]
    return lax.ppermute(value, axis, route)


def widen_lon(value):
    last = value[..., value.shape[-1] - HALO :]
    leading = value[..., :HALO]
    return jnp.concatenate([cyc(last, "lon", 1), value, cyc(leading, "lon", -1)], axis=-1)


def crop(value, ring):
    return value[..., ring : value.shape[-2] - ring, ring : value.shape[-1] - ring]


def sides(value):
    inner = value[..., 1:-1, 1:-1]
    east = value[..., 1:-1, 2:]
    west = value[..., 1:-1, :-2]
    north = value[..., 2:, 1:-1]
    south = value[..., :-2, 1:-1]
    return inner, east, west, north, south


def tangent(field, flow, sea):
    cu, cv = crop(flow[0], 1), crop(flow[1], 1)
    inner, east, west, north, south = sides(field)
    return crop(sea, 1) * (
        (1.0 - 4.0 * NU) * inner
        + (NU - 0.5 * cu) * east
        + (NU + 0.5 * cu) * west
        + (NU - 0.5 * cv) * north
        + (NU + 0.5 * cv) * south
    )


def adjoint(field, flow, sea):
    masked = sea * field
    summed = (1.0 - 4.0 * NU) * sides(masked)[0]
    summed = summed + sides((NU - 0.5 * flow[0]) * masked)[2]
    summed = summed + sides((NU + 0.5 * flow[0]) * masked)[1]
    summed = summed + sides((NU - 0.5 * flow[1]) * masked)[4]
    summed = summed + sides((NU + 0.5 * flow[1]) * masked)[3]
    return summed


def local(
    ens_control, perturbations, zonal_control, spread, currents, sea_mask, observed, loc_reach
):
    bands = lax.axis_size("lat")
    members = ens_control.shape[0]
    group = members // loc_reach.shape[0]
    rows = spread.shape[2]
    scale = 1.0 / math.sqrt(members - 1)
    zscale = 1.0 / math.sqrt(ens_control.shape[4] * lax.axis_size("lon"))
    distance_axis = jnp.arange(3).astype(jnp.float32)
    limits = loc_reach.astype(jnp.float32)[:, None] + 1.0
    block_weights = jnp.maximum(0.0, 1.0 - distance_axis[None, :] / limits)
    weights = jnp.repeat(block_weights, group, axis=0)

    pert = {0: perturbations}
    for o in (1, -1, 2, -2):
        pert[o] = cyc(perturbations, "lat", -o)

    sea_f = sea_mask.astype(jnp.float32)
    inputs = jnp.concatenate(
        [
            currents.reshape((-1,) + currents.shape[-2:]),
            observed.reshape((-1,) + observed.shape[-2:]),
            sea_f[None],
        ],
        axis=0,
    )
    inputs = widen_lon(inputs)
    inputs = jnp.concatenate(
        [open_step(inputs, "lat", 1), inputs, open_step(inputs, "lat", -1)], axis=-2
    )
    ncur = currents.shape[0] * currents.shape[1]
    flow = inputs[:ncur].reshape(currents.shape[:2] + inputs.shape[1:])
    obs = inputs[ncur:-1].reshape(observed.shape[:3] + inputs.shape[1:])
    sea = inputs[-1]

    def pair(o):
        w = weights[:, abs(o)][:, None, None, None, None] * scale
        return jnp.sum(
            w * pert[o].astype(jnp.float32) * ens_control.astype(jnp.float32), axis=0
        )

    part = {o: pair(o) for o in range(-2, 3)}
    part[0] = part[0] + spread * zonal_control[..., None] * zscale
    sums = {s: part[s] for s in (-1, 0, 1)}
    for d in (1, -1, 2, -2, 3, -3):
        which = [s for s in (-1, 0, 1) if abs(d + s) <= 2]
        moved = cyc(jnp.stack([part[d + s] for s in which]), "lat", d)
        for n, s in enumerate(which):
            sums[s] = sums[s] + moved[n]
    band = lax.axis_index("lat")
    south = jnp.where(band > 0, sums[-1], 0.0)
    north = jnp.where(band < bands - 1, sums[1], 0.0)
    start = jnp.concatenate([south, sums[0], north], axis=2)
    start = widen_lon(start)

    first = tangent(start, flow, sea)
    second = tangent(first, crop(flow, 1), crop(sea, 1))
    weighted = crop(first, 2) - crop(obs[0], 3) + adjoint(
        second - crop(obs[1], 2), crop(flow, 2), crop(sea, 2)
    )
    sensitivity = adjoint(weighted, crop(flow, 3), crop(sea, 3))

    grad = None
    for o in (0, 1, -1, 2, -2):
        sens = sensitivity if o == 0 else cyc(sensitivity, "lat", -o)
        product = (pert[o].astype(jnp.float32) * sens * scale).astype(jnp.bfloat16)
        term = weights[:, abs(o)][:, None, None, None, None] * product.astype(jnp.float32)
        grad = term if grad is None else grad + term
    zonal_part = jnp.sum(spread * sensitivity, axis=3)
    summed = lax.psum(zonal_part.reshape(1, -1), "lon").reshape(zonal_part.shape)
    zonal_grad = zonal_control + summed * zscale
    return grad, zonal_grad


def solution(mesh):
    return jax.shard_map(
        local,
        mesh=mesh,
        in_specs=(
            P(None, None, None, "lat", "lon"),
            P(None, None, None, "lat", "lon"),
            P(None, None, "lat"),
            P(None, None, "lat", "lon"),
            P(None, None, "lat", "lon"),
            P("lat", "lon"),
            P(None, None, None, "lat", "lon"),
            P(),
        ),
        out_specs=(P(None, None, None, "lat", "lon"), P(None, None, "lat")),
        check_vma=False,
    )
```

time: 284 us -> 282 us (level)
  the two profiles are of different devices: /device:TPU:23 before, /device:TPU:1 now
where the time goes in v1:
time: 282 us; the launch traced here: 277 us
  blocking collectives  116 us (41%)
  starting transfers between devices  109 us (39%)
  waiting for transfers between devices  31.3 us (11%)
  other arithmetic  17.3 us (6%)
    psum x1, blocking collectives, local(): lax.psum(zonal_part.reshape(1, -1), 'lon').reshape(zonal_part.shape)  116 us
    ppermute x18, starting transfers between devices, cyc(): lax.ppermute(value, axis, [((i - distance) % peers, i) for i in range(pee...  104 us
    ppermute x18, waiting for transfers between devices, cyc(): lax.ppermute(value, axis, [((i - distance) % peers, i) for i in range(pee...  29.7 us
  transfers between devices with their start and end apart: 20, of which 5 were waited for; matrix products, arithmetic and copies ran while one was open for 3% of the time, Pallas kernels for 0%

profile of v1, /device:TPU:1, one launch (start us, length us, event | category | flops | bytes accessed | tf_op | source)
XLA Modules:
  0.0 277.1 jit_solution(14051644287910937929)
XLA Ops:
  0.6 8.9 %collective-permute-start.5 = (bf16[64,3,4,4,128]{4,3,2,1,0:T(4,128)(2,1)}, bf16[64,3,4,4,128]{4,3,2,1,0:T(4,128)(2,1)S(1)}, u32[]{:S(2)}, u32[]{:S(2)}) collective-permute-start(bf16[64,3,4,4,128]{4,3,2,1,0:T(4,128)(2,1)} %param.9), channel_id=1, source_target_pairs={{64,0},{128,64},{192,128},{256,192},{320,256},{384,320},{448,384},... | collective-permute-start | bytes 2359304 | tf_op jit(solution)/shard_map/ppermute | solution.py:14
  9.5 1.9 collective-permute-start.4
  11.5 1.9 collective-permute-start.8
  13.4 0.7 convert_bitcast_fusion
  14.1 0.8 pad_maximum_fusion.8
  15.0 4.8 %collective-permute-start = (f32[33,4,4]{2,1,0:T(4,128)S(1)}, f32[33,4,4]{2,1,0:T(4,128)S(1)}, u32[]{:S(2)}, u32[]{:S(2)}) collective-permute-start(f32[33,4,4]{2,1,0:T(4,128)S(1)} %get-tuple-element.32), channel_id=1, source_target_pairs={{63,0},{0,1},{1,2},{2,3},{3,4},{4,5},{5,6},{6,7},{7,8},{8,9},{9,10... | collective-permute-start | bytes 6344 | tf_op jit(solution)/shard_map/ppermute | solution.py:14
  19.9 8.1 %collective-permute-start.1 = (f32[33,4,4]{2,1,0:T(4,128)S(1)}, f32[33,4,4]{2,1,0:T(4,128)S(1)}, u32[]{:S(2)}, u32[]{:S(2)}) collective-permute-start(f32[33,4,4]{2,1,0:T(4,128)S(1)} %get-tuple-element.33), channel_id=1, source_target_pairs={{1,0},{2,1},{3,2},{4,3},{5,4},{6,5},{7,6},{8,7},{9,8},{10,9},{11,1... | collective-permute-start | bytes 6344 | tf_op jit(solution)/shard_map/ppermute | solution.py:14
  29.5 1.0 pad_maximum_fusion.3
  30.5 1.3 collective-permute-start.3
  31.8 4.0 %collective-permute-start.2 = (f32[33,4,136]{2,1,0:T(4,128)S(1)}, f32[33,4,136]{2,1,0:T(4,128)S(1)}, u32[]{:S(2)}, u32[]{:S(2)}) collective-permute-start(f32[33,4,136]{2,1,0:T(4,128)S(1)} %pad_maximum_fusion.3), channel_id=1, source_target_pairs={{0,64},{64,128},{128,192},{192,256},{256,320},{320,384},{384,448},... | collective-permute-start | bytes 215432 | tf_op jit(solution)/shard_map/ppermute | solution.py:20
  36.4 1.6 collective-permute-done.3
  38.0 6.7 %collective-permute-start.6 = (bf16[64,3,4,4,128]{4,3,2,1,0:T(4,128)(2,1)}, bf16[64,3,4,4,128]{4,3,2,1,0:T(4,128)(2,1)S(1)}, u32[]{:S(2)}, u32[]{:S(2)}) collective-permute-start(bf16[64,3,4,4,128]{4,3,2,1,0:T(4,128)(2,1)} %param.9), channel_id=1, source_target_pairs={{128,0},{192,64},{256,128},{320,192},{384,256},{448,320},{512,384}... | collective-permute-start | bytes 2359304 | tf_op jit(solution)/shard_map/ppermute | solution.py:14
  44.7 0.8 pad_maximum_fusion.4
  45.8 1.2 pad_maximum_fusion
  47.5 27.7 %collective-permute-done.6 = bf16[64,3,4,4,128]{4,3,2,1,0:T(4,128)(2,1)S(1)} collective-permute-done((bf16[64,3,4,4,128]{4,3,2,1,0:T(4,128)(2,1)}, bf16[64,3,4,4,128]{4,3,2,1,0:T(4,128)(2,1)S(1)}, u32[]{:S(2)}, u32[]{:S(2)}) %collective-permute-start.6) | collective-permute-done | bytes 786464 | tf_op jit(solution)/shard_map/ppermute | solution.py:14
  75.3 3.2 %fusion.13 = (f32[3,4,4,128]{3,2,1,0:T(4,128)S(1)}, f32[3,4,4,128]{3,2,1,0:T(4,128)S(1)}, f32[3,4,4,128]{3,2,1,0:T(4,128)S(1)}, f32[3,4,4,128]{3,2,1,0:T(4,128)S(1)}, f32[3,4,4,128]{3,2,1,0:T(4,128)S(1)}) fusion(bf16[64,3,4,4,128]{4,3,2,1,0:T(4,128)(2,1)S(1)} %copy-done.5, bf16[64,3,4,4,128]{4,3,2,1,0:T(4,128)(2,1)S(1)} %collective-permute-done.6, ...), kind=kLoop, calls=%fused_computation.28 | loop fusion | flops 8226816 | bytes 4842240 | tf_op jit(solution)/shard_map/reduce_sum | solution.py:102
  78.5 22.4 %collective-permute-start.13 = (f32[1,3,4,4,128]{4,3,2,1,0:T(4,128)S(1)}, f32[1,3,4,4,128]{4,3,2,1,0:T(4,128)S(1)}, u32[]{:S(2)}, u32[]{:S(2)}) collective-permute-start(f32[1,3,4,4,128]{4,3,2,1,0:T(4,128)S(1)} %bitcast.141), channel_id=1, source_target_pairs={{192,0},{256,64},{320,128},{384,192},{448,256},{512,320},{576,384}... | collective-permute-start | bytes 73736 | tf_op jit(solution)/shard_map/ppermute | solution.py:14
  101.0 1.9 collective-permute-start.11
  103.0 2.8 %collective-permute-start.10 = (f32[2,3,4,4,128]{4,3,2,1,0:T(4,128)S(1)}, f32[2,3,4,4,128]{4,3,2,1,0:T(4,128)S(1)}, u32[]{:S(2)}, u32[]{:S(2)}) collective-permute-start(f32[2,3,4,4,128]{4,3,2,1,0:T(4,128)S(1)} %pad_maximum_fusion.9), channel_id=1, source_target_pairs={{896,0},{960,64},{0,128},{64,192},{128,256},{192,320},{256,384},{3... | collective-permute-start | bytes 147464 | tf_op jit(solution)/shard_map/ppermute | solution.py:14
  105.8 7.0 %collective-permute-start.12 = (f32[2,3,4,4,128]{4,3,2,1,0:T(4,128)S(1)}, f32[2,3,4,4,128]{4,3,2,1,0:T(4,128)S(1)}, u32[]{:S(2)}, u32[]{:S(2)}) collective-permute-start(f32[2,3,4,4,128]{4,3,2,1,0:T(4,128)S(1)} %pad_maximum_fusion.10), channel_id=1, source_target_pairs={{128,0},{192,64},{256,128},{320,192},{384,256},{448,320},{512,384}... | collective-permute-start | bytes 147464 | tf_op jit(solution)/shard_map/ppermute | solution.py:14
  112.9 1.9 collective-permute-start.7
  114.9 7.6 %collective-permute-start.9 = (f32[3,3,4,4,128]{4,3,2,1,0:T(4,128)S(1)}, f32[3,3,4,4,128]{4,3,2,1,0:T(4,128)S(1)}, u32[]{:S(2)}, u32[]{:S(2)}) collective-permute-start(f32[3,3,4,4,128]{4,3,2,1,0:T(4,128)S(1)} %get-tuple-element.39), channel_id=1, source_target_pairs={{64,0},{128,64},{192,128},{256,192},{320,256},{384,320},{448,384},... | collective-permute-start | bytes 221192 | tf_op jit(solution)/shard_map/ppermute | solution.py:14
  123.0 0.8 collective-permute-done.9
  124.1 4.3 %collective-permute-start.14 = (f32[3,4,12,4]{3,2,1,0:T(8,128)S(1)}, f32[3,4,12,4]{3,2,1,0:T(8,128)S(1)}, u32[]{:S(2)}, u32[]{:S(2)}) collective-permute-start(f32[3,4,12,4]{3,2,1,0:T(8,128)S(1)} %get-tuple-element.30), channel_id=1, source_target_pairs={{63,0},{0,1},{1,2},{2,3},{3,4},{4,5},{5,6},{6,7},{7,8},{8,9},{9,10... | collective-permute-start | bytes 6920 | tf_op jit(solution)/shard_map/ppermute | solution.py:14
  128.4 4.4 %collective-permute-start.15 = (f32[3,4,12,4]{3,2,1,0:T(8,128)S(1)}, f32[3,4,12,4]{3,2,1,0:T(8,128)S(1)}, u32[]{:S(2)}, u32[]{:S(2)}) collective-permute-start(f32[3,4,12,4]{3,2,1,0:T(8,128)S(1)} %get-tuple-element.31), channel_id=1, source_target_pairs={{1,0},{2,1},{3,2},{4,3},{5,4},{6,5},{7,6},{8,7},{9,8},{10,9},{11,1... | collective-permute-start | bytes 6920 | tf_op jit(solution)/shard_map/ppermute | solution.py:14
  133.6 0.7 collective-permute-done.15
  135.5 1.9 collective-permute-start.19
  137.4 7.9 %collective-permute-start.18 = (f32[3,4,4,128]{3,2,1,0:T(4,128)S(1)}, f32[3,4,4,128]{3,2,1,0:T(4,128)S(1)}, u32[]{:S(2)}, u32[]{:S(2)}) collective-permute-start(f32[3,4,4,128]{3,2,1,0:T(4,128)S(1)} %get-tuple-element.10), channel_id=1, source_target_pairs={{128,0},{192,64},{256,128},{320,192},{384,256},{448,320},{512,384}... | collective-permute-start | bytes 73736 | tf_op jit(solution)/shard_map/ppermute | solution.py:14
  145.3 2.8 %collective-permute-start.17 = (f32[3,4,4,128]{3,2,1,0:T(4,128)S(1)}, f32[3,4,4,128]{3,2,1,0:T(4,128)S(1)}, u32[]{:S(2)}, u32[]{:S(2)}) collective-permute-start(f32[3,4,4,128]{3,2,1,0:T(4,128)S(1)} %get-tuple-element.10), channel_id=1, source_target_pairs={{960,0},{0,64},{64,128},{128,192},{192,256},{256,320},{320,384},{3... | collective-permute-start | bytes 73736 | tf_op jit(solution)/shard_map/ppermute | solution.py:14
  148.1 6.7 %collective-permute-start.16 = (f32[3,4,4,128]{3,2,1,0:T(4,128)S(1)}, f32[3,4,4,128]{3,2,1,0:T(4,128)S(1)}, u32[]{:S(2)}, u32[]{:S(2)}) collective-permute-start(f32[3,4,4,128]{3,2,1,0:T(4,128)S(1)} %get-tuple-element.10), channel_id=1, source_target_pairs={{64,0},{128,64},{192,128},{256,192},{320,256},{384,320},{448,384},... | collective-permute-start | bytes 73736 | tf_op jit(solution)/shard_map/ppermute | solution.py:14
  154.9 116.0 %psum.7 = f32[1,48]{1,0:T(1,128)S(1)} all-reduce(f32[1,48]{1,0:T(1,128)S(1)} %reshape.83), channel_id=1, replica_groups=mesh['lat'=16,'lon'=64] {'lon'}, use_global_device_ids=true, to_apply=%region_6.7 | all-reduce | flops 48 | bytes 384 | tf_op jit(solution)/shard_map/psum | solution.py:134
  271.6 5.5 %multiply_add_fusion = f32[64,3,4,4,128]{4,3,2,1,0:T(4,128)} fusion(bf16[64,3,4,4,128]{4,3,2,1,0:T(4,128)(2,1)S(1)} %collective-permute-done.8, bf16[64,3,4,4,128]{4,3,2,1,0:T(4,128)(2,1)} %copy-done.1, bf16[64,3,4,4,128]{4,3,2,1,0:T(4,128)(2,1)S(1)} %collective-permute-done.5, bf16[64,3,4,4,128]{4,3,2,1,0:T(4,128)(2,1)S(1)} %collective-permute-done.4, ...), kind=kLoop, calls=%fused_computation.30 | loop fusion | flops 13369344 | bytes 5628672 | tf_op jit(solution)/shard_map/add | solution.py:132
  (95 shorter events, 6.4 us)
Async XLA Ops:
  0.6 46.9 %collective-permute-start.5 = (bf16[64,3,4,4,128]{4,3,2,1,0:T(4,128)(2,1)}, bf16[64,3,4,4,128]{4,3,2,1,0:T(4,128)(2,1)S(1)}, u32[]{:S(2)}, u32[]{:S(2)}) collective-permute-start(bf16[64,3,4,4,128]{4,3,2,1,0:T(4,128)(2,1)} %param.9), channel_id=1, source_target_pairs={{64,0},{128,64},{192,128},{256,192},{320,256},{384,320},{448,384},... | collective-permute-start | bytes 2359304 | tf_op jit(solution)/shard_map/ppermute | solution.py:14
  9.5 38.0 %collective-permute-start.4 = (bf16[64,3,4,4,128]{4,3,2,1,0:T(4,128)(2,1)}, bf16[64,3,4,4,128]{4,3,2,1,0:T(4,128)(2,1)S(1)}, u32[]{:S(2)}, u32[]{:S(2)}) collective-permute-start(bf16[64,3,4,4,128]{4,3,2,1,0:T(4,128)(2,1)} %param.9), channel_id=1, source_target_pairs={{960,0},{0,64},{64,128},{128,192},{192,256},{256,320},{320,384},{3... | collective-permute-start | bytes 2359304 | tf_op jit(solution)/shard_map/ppermute | solution.py:14
  11.5 36.0 %collective-permute-start.8 = (bf16[64,3,4,4,128]{4,3,2,1,0:T(4,128)(2,1)}, bf16[64,3,4,4,128]{4,3,2,1,0:T(4,128)(2,1)S(1)}, u32[]{:S(2)}, u32[]{:S(2)}) collective-permute-start(bf16[64,3,4,4,128]{4,3,2,1,0:T(4,128)(2,1)} %param.9), channel_id=1, source_target_pairs={{896,0},{960,64},{0,128},{64,192},{128,256},{192,320},{256,384},{3... | collective-permute-start | bytes 2359304 | tf_op jit(solution)/shard_map/ppermute | solution.py:14
  14.1 30.6 %copy-start.7 = (f32[1,4,128]{2,1,0:T(4,128)}, f32[1,4,128]{2,1,0:T(4,128)S(1)}, u32[]{:S(2)}) copy-start(f32[1,4,128]{2,1,0:T(4,128)S(1)} %convert_bitcast_fusion) | copy-start | bytes 6148
  15.0 14.5 %collective-permute-start = (f32[33,4,4]{2,1,0:T(4,128)S(1)}, f32[33,4,4]{2,1,0:T(4,128)S(1)}, u32[]{:S(2)}, u32[]{:S(2)}) collective-permute-start(f32[33,4,4]{2,1,0:T(4,128)S(1)} %get-tuple-element.32), channel_id=1, source_target_pairs={{63,0},{0,1},{1,2},{2,3},{3,4},{4,5},{5,6},{6,7},{7,8},{8,9},{9,10... | collective-permute-start | bytes 6344 | tf_op jit(solution)/shard_map/ppermute | solution.py:14
  19.9 9.7 %collective-permute-start.1 = (f32[33,4,4]{2,1,0:T(4,128)S(1)}, f32[33,4,4]{2,1,0:T(4,128)S(1)}, u32[]{:S(2)}, u32[]{:S(2)}) collective-permute-start(f32[33,4,4]{2,1,0:T(4,128)S(1)} %get-tuple-element.33), channel_id=1, source_target_pairs={{1,0},{2,1},{3,2},{4,3},{5,4},{6,5},{7,6},{8,7},{9,8},{10,9},{11,1... | collective-permute-start | bytes 6344 | tf_op jit(solution)/shard_map/ppermute | solution.py:14
  30.5 7.5 %collective-permute-start.3 = (f32[33,4,136]{2,1,0:T(4,128)S(1)}, f32[33,4,136]{2,1,0:T(4,128)S(1)}, u32[]{:S(2)}, u32[]{:S(2)}) collective-permute-start(f32[33,4,136]{2,1,0:T(4,128)S(1)} %pad_maximum_fusion.3), channel_id=1, source_target_pairs={{64,0},{128,64},{192,128},{256,192},{320,256},{384,320},{448,384},... | collective-permute-start | bytes 215432 | tf_op jit(solution)/shard_map/ppermute | solution.py:20
  31.8 12.9 %collective-permute-start.2 = (f32[33,4,136]{2,1,0:T(4,128)S(1)}, f32[33,4,136]{2,1,0:T(4,128)S(1)}, u32[]{:S(2)}, u32[]{:S(2)}) collective-permute-start(f32[33,4,136]{2,1,0:T(4,128)S(1)} %pad_maximum_fusion.3), channel_id=1, source_target_pairs={{0,64},{64,128},{128,192},{192,256},{256,320},{320,384},{384,448},... | collective-permute-start | bytes 215432 | tf_op jit(solution)/shard_map/ppermute | solution.py:20
  38.0 37.3 %collective-permute-start.6 = (bf16[64,3,4,4,128]{4,3,2,1,0:T(4,128)(2,1)}, bf16[64,3,4,4,128]{4,3,2,1,0:T(4,128)(2,1)S(1)}, u32[]{:S(2)}, u32[]{:S(2)}) collective-permute-start(bf16[64,3,4,4,128]{4,3,2,1,0:T(4,128)(2,1)} %param.9), channel_id=1, source_target_pairs={{128,0},{192,64},{256,128},{320,192},{384,256},{448,320},{512,384}... | collective-permute-start | bytes 2359304 | tf_op jit(solution)/shard_map/ppermute | solution.py:14
  45.6 29.7 %copy-start = (bf16[64,3,4,4,128]{4,3,2,1,0:T(4,128)(2,1)S(1)}, bf16[64,3,4,4,128]{4,3,2,1,0:T(4,128)(2,1)}, u32[]{:S(2)}) copy-start(bf16[64,3,4,4,128]{4,3,2,1,0:T(4,128)(2,1)} %param.9) | copy-start | bytes 2359300
  45.6 29.7 %copy-start.5 = (bf16[64,3,4,4,128]{4,3,2,1,0:T(4,128)(2,1)S(1)}, bf16[64,3,4,4,128]{4,3,2,1,0:T(4,128)(2,1)}, u32[]{:S(2)}) copy-start(bf16[64,3,4,4,128]{4,3,2,1,0:T(4,128)(2,1)} %param.8) | copy-start | bytes 2359300
  45.6 29.7 %copy-start.14 = (f32[64]{0:T(128)S(1)}, f32[64]{0:T(128)}, u32[]{:S(2)}) copy-start(f32[64]{0:T(128)} %get-tuple-element.43) | copy-start | bytes 772
  47.1 86.5 %copy-start.3 = (f32[33,12,136]{2,1,0:T(8,128)}, f32[33,12,136]{2,1,0:T(8,128)S(1)}, u32[]{:S(2)}) copy-start(f32[33,12,136]{2,1,0:T(8,128)S(1)} %pad_maximum_fusion) | copy-start | bytes 646276
  75.3 37.5 %copy-start.6 = (f32[3,4,4,128]{3,2,1,0:T(4,128)S(1)}, f32[3,4,4,128]{3,2,1,0:T(4,128)}, u32[]{:S(2)}) copy-start(f32[3,4,4,128]{3,2,1,0:T(4,128)} %param.11) | copy-start | bytes 73732
  75.3 37.5 %copy-start.9 = (f32[3,4,4]{2,1,0:T(4,128)S(1)}, f32[3,4,4]{2,1,0:T(4,128)}, u32[]{:S(2)}) copy-start(f32[3,4,4]{2,1,0:T(4,128)} %param.10) | copy-start | bytes 580
  75.3 47.1 %copy-start.8 = (f32[1,4,128]{2,1,0:T(4,128)S(1)}, f32[1,4,128]{2,1,0:T(4,128)}, u32[]{:S(2)}) copy-start(f32[1,4,128]{2,1,0:T(4,128)} %copy-done.7) | copy-start | bytes 6148
  78.5 36.3 %collective-permute-start.13 = (f32[1,3,4,4,128]{4,3,2,1,0:T(4,128)S(1)}, f32[1,3,4,4,128]{4,3,2,1,0:T(4,128)S(1)}, u32[]{:S(2)}, u32[]{:S(2)}) collective-permute-start(f32[1,3,4,4,128]{4,3,2,1,0:T(4,128)S(1)} %bitcast.141), channel_id=1, source_target_pairs={{192,0},{256,64},{320,128},{384,192},{448,256},{512,320},{576,384}... | collective-permute-start | bytes 73736 | tf_op jit(solution)/shard_map/ppermute | solution.py:14
  101.0 21.6 %collective-permute-start.11 = (f32[1,3,4,4,128]{4,3,2,1,0:T(4,128)S(1)}, f32[1,3,4,4,128]{4,3,2,1,0:T(4,128)S(1)}, u32[]{:S(2)}, u32[]{:S(2)}) collective-permute-start(f32[1,3,4,4,128]{4,3,2,1,0:T(4,128)S(1)} %bitcast.138), channel_id=1, source_target_pairs={{832,0},{896,64},{960,128},{0,192},{64,256},{128,320},{192,384},{2... | collective-permute-start | bytes 73736 | tf_op jit(solution)/shard_map/ppermute | solution.py:14
  103.0 19.7 %collective-permute-start.10 = (f32[2,3,4,4,128]{4,3,2,1,0:T(4,128)S(1)}, f32[2,3,4,4,128]{4,3,2,1,0:T(4,128)S(1)}, u32[]{:S(2)}, u32[]{:S(2)}) collective-permute-start(f32[2,3,4,4,128]{4,3,2,1,0:T(4,128)S(1)} %pad_maximum_fusion.9), channel_id=1, source_target_pairs={{896,0},{960,64},{0,128},{64,192},{128,256},{192,320},{256,384},{3... | collective-permute-start | bytes 147464 | tf_op jit(solution)/shard_map/ppermute | solution.py:14
  105.8 16.9 %collective-permute-start.12 = (f32[2,3,4,4,128]{4,3,2,1,0:T(4,128)S(1)}, f32[2,3,4,4,128]{4,3,2,1,0:T(4,128)S(1)}, u32[]{:S(2)}, u32[]{:S(2)}) collective-permute-start(f32[2,3,4,4,128]{4,3,2,1,0:T(4,128)S(1)} %pad_maximum_fusion.10), channel_id=1, source_target_pairs={{128,0},{192,64},{256,128},{320,192},{384,256},{448,320},{512,384}... | collective-permute-start | bytes 147464 | tf_op jit(solution)/shard_map/ppermute | solution.py:14
  112.9 10.1 %collective-permute-start.7 = (f32[3,3,4,4,128]{4,3,2,1,0:T(4,128)S(1)}, f32[3,3,4,4,128]{4,3,2,1,0:T(4,128)S(1)}, u32[]{:S(2)}, u32[]{:S(2)}) collective-permute-start(f32[3,3,4,4,128]{4,3,2,1,0:T(4,128)S(1)} %get-tuple-element.38), channel_id=1, source_target_pairs={{960,0},{0,64},{64,128},{128,192},{192,256},{256,320},{320,384},{3... | collective-permute-start | bytes 221192 | tf_op jit(solution)/shard_map/ppermute | solution.py:14
  114.9 9.0 %collective-permute-start.9 = (f32[3,3,4,4,128]{4,3,2,1,0:T(4,128)S(1)}, f32[3,3,4,4,128]{4,3,2,1,0:T(4,128)S(1)}, u32[]{:S(2)}, u32[]{:S(2)}) collective-permute-start(f32[3,3,4,4,128]{4,3,2,1,0:T(4,128)S(1)} %get-tuple-element.39), channel_id=1, source_target_pairs={{64,0},{128,64},{192,128},{256,192},{320,256},{384,320},{448,384},... | collective-permute-start | bytes 221192 | tf_op jit(solution)/shard_map/ppermute | solution.py:14
  124.1 9.5 %collective-permute-start.14 = (f32[3,4,12,4]{3,2,1,0:T(8,128)S(1)}, f32[3,4,12,4]{3,2,1,0:T(8,128)S(1)}, u32[]{:S(2)}, u32[]{:S(2)}) collective-permute-start(f32[3,4,12,4]{3,2,1,0:T(8,128)S(1)} %get-tuple-element.30), channel_id=1, source_target_pairs={{63,0},{0,1},{1,2},{2,3},{3,4},{4,5},{5,6},{6,7},{7,8},{8,9},{9,10... | collective-permute-start | bytes 6920 | tf_op jit(solution)/shard_map/ppermute | solution.py:14
  128.4 5.9 %collective-permute-start.15 = (f32[3,4,12,4]{3,2,1,0:T(8,128)S(1)}, f32[3,4,12,4]{3,2,1,0:T(8,128)S(1)}, u32[]{:S(2)}, u32[]{:S(2)}) collective-permute-start(f32[3,4,12,4]{3,2,1,0:T(8,128)S(1)} %get-tuple-element.31), channel_id=1, source_target_pairs={{1,0},{2,1},{3,2},{4,3},{5,4},{6,5},{7,6},{8,7},{9,8},{10,9},{11,1... | collective-permute-start | bytes 6920 | tf_op jit(solution)/shard_map/ppermute | solution.py:14
  134.5 136.5 %copy-start.10 = (f32[3,4,4]{2,1,0:T(4,128)S(1)}, f32[3,4,4]{2,1,0:T(4,128)}, u32[]{:S(2)}) copy-start(f32[3,4,4]{2,1,0:T(4,128)} %param.10) | copy-start | bytes 580
  134.5 137.1 %copy-start.11 = (f32[64]{0:T(128)S(1)}, f32[64]{0:T(128)}, u32[]{:S(2)}) copy-start(f32[64]{0:T(128)} %get-tuple-element.40) | copy-start | bytes 772
  134.5 137.1 %copy-start.12 = (f32[64]{0:T(128)S(1)}, f32[64]{0:T(128)}, u32[]{:S(2)}) copy-start(f32[64]{0:T(128)} %get-tuple-element.41) | copy-start | bytes 772
  134.5 137.1 %copy-start.13 = (f32[64]{0:T(128)S(1)}, f32[64]{0:T(128)}, u32[]{:S(2)}) copy-start(f32[64]{0:T(128)} %get-tuple-element.42) | copy-start | bytes 772
  135.5 136.1 %collective-permute-start.19 = (f32[3,4,4,128]{3,2,1,0:T(4,128)S(1)}, f32[3,4,4,128]{3,2,1,0:T(4,128)S(1)}, u32[]{:S(2)}, u32[]{:S(2)}) collective-permute-start(f32[3,4,4,128]{3,2,1,0:T(4,128)S(1)} %get-tuple-element.10), channel_id=1, source_target_pairs={{896,0},{960,64},{0,128},{64,192},{128,256},{192,320},{256,384},{3... | collective-permute-start | bytes 73736 | tf_op jit(solution)/shard_map/ppermute | solution.py:14
  137.4 134.2 %collective-permute-start.18 = (f32[3,4,4,128]{3,2,1,0:T(4,128)S(1)}, f32[3,4,4,128]{3,2,1,0:T(4,128)S(1)}, u32[]{:S(2)}, u32[]{:S(2)}) collective-permute-start(f32[3,4,4,128]{3,2,1,0:T(4,128)S(1)} %get-tuple-element.10), channel_id=1, source_target_pairs={{128,0},{192,64},{256,128},{320,192},{384,256},{448,320},{512,384}... | collective-permute-start | bytes 73736 | tf_op jit(solution)/shard_map/ppermute | solution.py:14
  145.3 126.3 %collective-permute-start.17 = (f32[3,4,4,128]{3,2,1,0:T(4,128)S(1)}, f32[3,4,4,128]{3,2,1,0:T(4,128)S(1)}, u32[]{:S(2)}, u32[]{:S(2)}) collective-permute-start(f32[3,4,4,128]{3,2,1,0:T(4,128)S(1)} %get-tuple-element.10), channel_id=1, source_target_pairs={{960,0},{0,64},{64,128},{128,192},{192,256},{256,320},{320,384},{3... | collective-permute-start | bytes 73736 | tf_op jit(solution)/shard_map/ppermute | solution.py:14
  148.1 123.5 %collective-permute-start.16 = (f32[3,4,4,128]{3,2,1,0:T(4,128)S(1)}, f32[3,4,4,128]{3,2,1,0:T(4,128)S(1)}, u32[]{:S(2)}, u32[]{:S(2)}) collective-permute-start(f32[3,4,4,128]{3,2,1,0:T(4,128)S(1)} %get-tuple-element.10), channel_id=1, source_target_pairs={{64,0},{128,64},{192,128},{256,192},{320,256},{384,320},{448,384},... | collective-permute-start | bytes 73736 | tf_op jit(solution)/shard_map/ppermute | solution.py:14
  (6 other events, 85.5 us)

commit v2 on v1

v2 whole, which is shorter than its diff:
```python
import math

import jax
import jax.numpy as jnp
from jax import lax
from jax.experimental import pallas as pl
from jax.experimental.pallas import tpu as pltpu
from jax.sharding import PartitionSpec as P

NU = 0.2
REACH = 2
HALO = 4
PAD = 16
LANES = 128
PACK = LANES // HALO
LEAST = 3
FEW = 4
VMEM = pltpu.MemorySpace.VMEM
SMEM = pltpu.MemorySpace.SMEM


def shift(value, axis, distance):
    peers = lax.axis_size(axis)
    return lax.ppermute(value, axis, [((i - distance) % peers, i) for i in range(peers)])


def pairs_kernel(order, count, weight, own, control, up1, down1, up2, down2, out):
    i = pl.program_id(0)

    def add(slot, source, w):
        total = None
        for m in range(control.shape[1]):
            term = source[0, m].astype(jnp.float32) * control[0, m].astype(jnp.float32)
            total = term if total is None else total + term
        out[slot] += w * total

    @pl.when(i == 0)
    def _():
        out[...] = jnp.zeros(out.shape, out.dtype)

    add(2, own, weight[i, 0])

    @pl.when(i < count[0])
    def _():
        add(3, up1, weight[i, 1])
        add(1, down1, weight[i, 1])

    @pl.when(i < count[1])
    def _():
        add(4, up2, weight[i, 2])
        add(0, down2, weight[i, 2])


def mixed_kernel(rank, weight, sens, own, up1, down1, up2, down2, out):
    j = pl.program_id(0)

    def product(source, slot, m):
        value = source[0, m].astype(jnp.float32) * sens[slot]
        return value.astype(jnp.bfloat16).astype(jnp.float32)

    for m in range(own.shape[1]):
        out[0, m] = weight[j, 0] * product(own, 2, m)

    @pl.when(weight[j, 1] > 0.0)
    def _():
        for m in range(own.shape[1]):
            out[0, m] += weight[j, 1] * (product(up1, 3, m) + product(down1, 1, m))

    @pl.when(weight[j, 2] > 0.0)
    def _():
        for m in range(own.shape[1]):
            out[0, m] += weight[j, 2] * (product(up2, 4, m) + product(down2, 0, m))


def lane(shape):
    return lax.broadcasted_iota(jnp.int32, shape, len(shape) - 1)


def gather_kernel(inside, part, inputs, r1, m1, r2, m2, r3, m3, field, west_edge, east_edge):
    n = r3.shape[0]
    south = part[n : 2 * n] + r1[:n] + m1[:n] + r2[:n] + r3[...]
    mid = part[2 * n : 3 * n] + r1[n : 2 * n] + m1[n : 2 * n] + r2[n : 2 * n] + m2[:n]
    north = part[3 * n : 4 * n] + r1[2 * n : 3 * n] + m1[2 * n : 3 * n] + m2[n : 2 * n] + m3[...]
    low, high = inside[0] > 0, inside[1] > 0
    field[:, 12:PAD] = jnp.zeros((field.shape[0], PAD - 12, LANES), jnp.float32)
    field[:n, 0:4] = jnp.where(low, south, 0.0)
    field[:n, 4:8] = mid
    field[:n, 8:12] = jnp.where(high, north, 0.0)
    field[n:, 0:4] = jnp.where(low, r1[3 * n :], 0.0)
    field[n:, 4:8] = inputs[...]
    field[n:, 8:12] = jnp.where(high, m1[3 * n :], 0.0)
    spot = lane((PAD, LANES)) // HALO
    for g in range(west_edge.shape[0]):
        west = jnp.zeros((PAD, LANES), jnp.float32)
        east = jnp.zeros((PAD, LANES), jnp.float32)
        for k in range(min(PACK, field.shape[0] - g * PACK)):
            value = field[g * PACK + k]
            at = HALO * k
            west = jnp.where(spot == k, pltpu.roll(value, at, 1) if at else value, west)
            east = jnp.where(spot == k, pltpu.roll(value, (at + HALO) % LANES, 1) if at + HALO < LANES else value, east)
        west_edge[g] = west
        east_edge[g] = east


def stencil_kernel(field, from_east, from_west, out):
    n = out.shape[0]
    cols = lane((PAD, LANES))

    def turn(value, amount):
        return pltpu.roll(value, amount % LANES, 1) if amount % LANES else value

    def wide(i):
        g, at = i // PACK, HALO * (i % PACK)
        right = turn(from_east[g], -at)
        left = turn(from_west[g], -at - HALO)
        beside = jnp.where(cols < HALO, right, jnp.where(cols >= LANES - HALO, left, 0.0))
        return field[i], beside

    def at_west(v):
        a, b = pltpu.roll(v[0], 1, 1), pltpu.roll(v[1], 1, 1)
        return jnp.where(cols == 0, b, a), jnp.where(cols == 0, a, b)

    def at_east(v):
        a, b = pltpu.roll(v[0], LANES - 1, 1), pltpu.roll(v[1], LANES - 1, 1)
        return jnp.where(cols == LANES - 1, b, a), jnp.where(cols == LANES - 1, a, b)

    def at_north(v):
        return tuple(pltpu.roll(x, PAD - 1, 0) for x in v)

    def at_south(v):
        return tuple(pltpu.roll(x, 1, 0) for x in v)

    def each(f, *vs):
        return tuple(f(*xs) for xs in zip(*vs))

    def mul(a, b):
        return each(lambda x, y: x * y, a, b)

    def sub(a, b):
        return each(lambda x, y: x - y, a, b)

    def total(*vs):
        return each(lambda *xs: sum(xs[1:], xs[0]), *vs)

    centre = 1.0 - 4.0 * NU
    levels = n // 3
    sea = wide(field.shape[0] - 1)
    for l in range(levels):
        cu, cv = wide(n + l), wide(n + levels + l)
        east_c = each(lambda x: NU - 0.5 * x, cu)
        west_c = each(lambda x: NU + 0.5 * x, cu)
        north_c = each(lambda x: NU - 0.5 * x, cv)
        south_c = each(lambda x: NU + 0.5 * x, cv)

        def tangent(f):
            return mul(
                sea,
                total(
                    each(lambda x: centre * x, f),
                    mul(east_c, at_east(f)),
                    mul(west_c, at_west(f)),
                    mul(north_c, at_north(f)),
                    mul(south_c, at_south(f)),
                ),
            )

        def adjoint(f):
            z = mul(sea, f)
            return total(
                each(lambda x: centre * x, z),
                at_west(mul(east_c, z)),
                at_east(mul(west_c, z)),
                at_south(mul(north_c, z)),
                at_north(mul(south_c, z)),
            )

        for t in range(3):
            i = t * levels + l
            first = tangent(wide(i))
            second = tangent(first)
            near = wide(n + 2 * levels + i)
            later = wide(n + 2 * levels + n + i)
            weighted = total(sub(first, near), adjoint(sub(second, later)))
            out[i] = adjoint(weighted)[0][4:8]


def whole():
    return pl.BlockSpec(memory_space=VMEM)


def local(
    ens_control, perturbations, zonal_control, spread, currents, sea_mask, observed, loc_reach
):
    bands = lax.axis_size("lat")
    slabs = lax.axis_size("lon")
    members, tracers, levels, rows, columns = ens_control.shape
    blocks = loc_reach.shape[0]
    group = members // blocks
    cells = tracers * levels * rows
    scale = 1.0 / math.sqrt(members - 1)
    zscale = 1.0 / math.sqrt(columns * slabs)
    limits = loc_reach.astype(jnp.float32)[:, None] + 1.0
    weights = jnp.maximum(0.0, 1.0 - jnp.arange(REACH + 1).astype(jnp.float32)[None, :] / limits)

    mine, other = loc_reach[:, None], loc_reach[None, :]
    index = jnp.arange(blocks)
    ahead = (other > mine) | ((other == mine) & (index[None, :] < index[:, None]))
    rank = jnp.sum(ahead.astype(jnp.int32), axis=1)
    placed = rank[None, :] == index[:, None]
    order = jnp.sum(jnp.where(placed, index[None, :], 0), axis=1).astype(jnp.int32)
    sorted_weights = jnp.sum(jnp.where(placed[:, :, None], weights[None], 0.0), axis=1)
    count1 = jnp.sum((loc_reach >= 1).astype(jnp.int32))
    count2 = jnp.sum((loc_reach >= 2).astype(jnp.int32))

    own = perturbations.reshape(blocks, group, cells, columns)
    control = ens_control.reshape(blocks, group, cells, columns)
    sending = lax.optimization_barrier(jnp.take(own, order, axis=0, mode="clip"))
    most = blocks - 1

    def exchange(near, far):
        def run(block):
            got = []
            for distance, n in ((-1, near), (1, near), (-2, far), (2, far)):
                moved = shift(block[:n], "lat", distance)
                rest = jnp.zeros((most - n,) + block.shape[1:], block.dtype)
                got.append(jnp.concatenate([moved, rest], axis=0) if n < most else moved)
            return tuple(got)

        return run

    sizes, starts = [], []
    for near in range(LEAST, most + 1):
        starts.append(len(sizes))
        far = list(range(2, min(near, FEW) + 1))
        sizes += [(near, n) for n in far + [near] * (near > FEW)]
    cases = [exchange(near, far) for near, far in sizes]
    near = jnp.maximum(count1, LEAST)
    case = jnp.clip(count2 - 2, 0, FEW - 1)
    for n, first in enumerate(starts):
        case = case + jnp.where(near == LEAST + n, first, 0)
    up1, down1, up2, down2 = lax.optimization_barrier(lax.switch(case, cases, sending))

    block = (1, group, cells, columns)
    place = pl.BlockSpec(block, lambda i, order, count: (order[i], 0, 0, 0))
    got = pl.BlockSpec(block, lambda i, order, count: (jnp.minimum(i, most - 1), 0, 0, 0))
    part = pl.pallas_call(
        pairs_kernel,
        grid_spec=pltpu.PrefetchScalarGridSpec(
            num_scalar_prefetch=2,
            grid=(blocks,),
            in_specs=[pl.BlockSpec(memory_space=SMEM), place, place, got, got, got, got],
            out_specs=pl.BlockSpec((5, cells, columns), lambda i, order, count: (0, 0, 0)),
        ),
        out_shape=jax.ShapeDtypeStruct((5, cells, columns), jnp.float32),
        name="pairs",
    )(order, jnp.stack([count1, count2]), sorted_weights * scale, own, control, up1, down1, up2, down2)

    items = tracers * levels
    part = part.reshape(5, items, rows, columns)
    prior = (spread * zonal_control[..., None] * zscale).reshape(items, rows, columns)
    part = jnp.concatenate([part[:2], (part[2] + prior)[None], part[3:]], axis=0)
    part = part.reshape(5 * items, rows, columns)
    inputs = jnp.concatenate(
        [
            currents.reshape(-1, rows, columns),
            observed.reshape(-1, rows, columns),
            sea_mask.astype(jnp.float32)[None],
        ],
        axis=0,
    )
    r3 = shift(part[4 * items :], "lat", 3)
    m3 = shift(part[:items], "lat", -3)
    r2 = shift(part[3 * items :], "lat", 2)
    m2 = shift(part[: 2 * items], "lat", -2)
    r1 = shift(jnp.concatenate([part[2 * items :], inputs], axis=0), "lat", 1)
    m1 = shift(jnp.concatenate([part[: 3 * items], inputs], axis=0), "lat", -1)
    band = lax.axis_index("lat")
    inside = jnp.stack([band > 0, band < bands - 1]).astype(jnp.int32)
    total = items + inputs.shape[0]
    packs = -(-total // PACK)
    field, west_edge, east_edge = pl.pallas_call(
        gather_kernel,
        in_specs=[pl.BlockSpec(memory_space=SMEM)] + [whole()] * 8,
        out_specs=[whole()] * 3,
        out_shape=[
            jax.ShapeDtypeStruct((total, PAD, columns), jnp.float32),
            jax.ShapeDtypeStruct((packs, PAD, columns), jnp.float32),
            jax.ShapeDtypeStruct((packs, PAD, columns), jnp.float32),
        ],
        name="gather",
    )(inside, part, inputs, r1, m1, r2, m2, r3, m3)
    from_east = shift(west_edge, "lon", -1)
    from_west = shift(east_edge, "lon", 1)
    sensitivity = pl.pallas_call(
        stencil_kernel,
        in_specs=[whole()] * 3,
        out_specs=whole(),
        out_shape=jax.ShapeDtypeStruct((items, rows, columns), jnp.float32),
        name="stencil",
    )(field, from_east, from_west)

    down = [shift(sensitivity, "lat", d) for d in (2, 1)]
    up = [shift(sensitivity, "lat", -d) for d in (1, 2)]
    sens = jnp.stack(down + [sensitivity] + up).reshape(5, cells, columns) * scale

    zonal_part = jnp.sum(spread.reshape(cells, columns) * sensitivity.reshape(cells, columns), axis=1)
    spread_out = jnp.broadcast_to(zonal_part[None], (slabs, cells))
    everyone = lax.all_to_all(spread_out, "lon", 0, 0, tiled=True)
    summed = jnp.sum(everyone, axis=0).reshape(zonal_control.shape)
    zonal_grad = zonal_control + summed * zscale

    here = pl.BlockSpec(block, lambda j, rank: (j, 0, 0, 0))
    taken = pl.BlockSpec(block, lambda j, rank: (jnp.minimum(rank[j], most - 1), 0, 0, 0))
    grad = pl.pallas_call(
        mixed_kernel,
        grid_spec=pltpu.PrefetchScalarGridSpec(
            num_scalar_prefetch=1,
            grid=(blocks,),
            in_specs=[
                pl.BlockSpec(memory_space=SMEM),
                pl.BlockSpec((5, cells, columns), lambda j, rank: (0, 0, 0)),
                here,
                taken,
                taken,
                taken,
                taken,
            ],
            out_specs=here,
        ),
        out_shape=jax.ShapeDtypeStruct((blocks, group, cells, columns), jnp.float32),
        name="mixed",
    )(rank, weights, sens, own, up1, down1, up2, down2)
    return grad.reshape(ens_control.shape), zonal_grad


def solution(mesh):
    return jax.shard_map(
        local,
        mesh=mesh,
        in_specs=(
            P(None, None, None, "lat", "lon"),
            P(None, None, None, "lat", "lon"),
            P(None, None, "lat"),
            P(None, None, "lat", "lon"),
            P(None, None, "lat", "lon"),
            P("lat", "lon"),
            P(None, None, None, "lat", "lon"),
            P(),
        ),
        out_specs=(P(None, None, None, "lat", "lon"), P(None, None, "lat")),
        check_vma=False,
    )
```

time: 282 us -> 184 us (0.65); the launches traced: 277 us -> 185 us
  blocking collectives: 116 us -> 0 us
  waiting for transfers between devices: 31.3 us -> 59.7 us
  starting transfers between devices: 109 us -> 84.2 us
  Pallas kernels: 0 us -> 18.9 us
  local copies, waits for them, and re-layouts: 1.96 us -> 10.2 us
  other arithmetic: 17.3 us -> 10 us
    psum x1 -> x0, blocking collectives: 116 us -> none  [local(): lax.psum(zonal_part.reshape(1, -1), 'lon').reshape(zonal_part.shape)]
    ppermute x20 -> x16, starting transfers between devices: 109 us -> 71.4 us  [shift(): lax.ppermute(value, axis, [((i - distance) % peers, i) for i in range(pee...]
    ppermute x20 -> x16, waiting for transfers between devices: 31.3 us -> 55.2 us  [shift(): lax.ppermute(value, axis, [((i - distance) % peers, i) for i in range(pee...]
    pallas_call x0 -> x4, Pallas kernels: none -> 18.9 us  [the longest x1 7.32 us: local(): pl.pallas_call(mixed_kernel, grid_spec=pltpu.PrefetchScalarGridSpec(num_s...]
    all_to_all x0 -> x1, starting transfers between devices: none -> 12.8 us  [local(): everyone = lax.all_to_all(spread_out, 'lon', 0, 0, tiled=True)]
    add x2 -> x1, other arithmetic: 5.49 us -> 0.01 us  [local(): part[2] + prior]
    all_to_all x0 -> x1, waiting for transfers between devices: none -> 4.49 us  [local(): everyone = lax.all_to_all(spread_out, 'lon', 0, 0, tiled=True)]
    concatenate x0 -> x4, local copies, waits for them, and re-layouts: none -> 3.69 us  [run(): got.append(jnp.concatenate([moved, rest], axis=0) if n < most else moved)]
  transfers between devices with their start and end apart: 20 -> 17, of which waited for: 5 -> 6; matrix products, arithmetic and copies ran while one was open for 3% -> 4% of each run, Pallas kernels for 0% -> 4%
where the time goes in v2:
time: 184 us; the launch traced here: 185 us
  starting transfers between devices  84.2 us (46%)
  waiting for transfers between devices  59.7 us (32%)
  Pallas kernels  18.9 us (10%)
  local copies, waits for them, and re-layouts  10.2 us (6%)
  other arithmetic  10 us (5%)
  between operations  2.34 us (1%)
    ppermute x16, starting transfers between devices, shift(): lax.ppermute(value, axis, [((i - distance) % peers, i) for i in range(pee...  71.4 us
    ppermute x16, waiting for transfers between devices, shift(): lax.ppermute(value, axis, [((i - distance) % peers, i) for i in range(pee...  55.2 us
    all_to_all x1, starting transfers between devices, local(): everyone = lax.all_to_all(spread_out, 'lon', 0, 0, tiled=True)  12.8 us
    pallas_call x1, Pallas kernels, local(): pl.pallas_call(mixed_kernel, grid_spec=pltpu.PrefetchScalarGridSpec(num_s...  7.32 us
    pallas_call x1, Pallas kernels, local(): pl.pallas_call(pairs_kernel, grid_spec=pltpu.PrefetchScalarGridSpec(num_s...  6.38 us
    all_to_all x1, waiting for transfers between devices, local(): everyone = lax.all_to_all(spread_out, 'lon', 0, 0, tiled=True)  4.49 us
    concatenate x4, local copies, waits for them, and re-layouts, run(): got.append(jnp.concatenate([moved, rest], axis=0) if n < most else moved)  3.69 us
  transfers between devices with their start and end apart: 17, of which 6 were waited for; matrix products, arithmetic and copies ran while one was open for 4% of the time, Pallas kernels for 4%

profile of v2, /device:TPU:1, one launch (start us, length us, event | category | flops | bytes accessed | tf_op | source)
XLA Modules:
  0.0 185.5 jit_solution(6419701933239917626)
XLA Ops:
  0.6 1.3 fusion.3
  5.0 1.8 gather_fusion
  6.9 58.6 %conditional.1 = (bf16[7,8,48,128]{3,2,1,0:T(8,128)(2,1)}, bf16[7,8,48,128]{3,2,1,0:T(8,128)(2,1)}, bf16[7,8,48,128]{3,2,1,0:T(8,128)(2,1)}, bf16[7,8,48,128]{3,2,1,0:T(8,128)(2,1)}) conditional(s32[]{:T(128)} %clamp.3, bf16[8,8,48,128]{3,2,1,0:T(8,128)(2,1)S(1)} %gather_fusion, ...), branch_computations={%region_5.6_spmd, %region_6.7_spmd, %region_7.8_spmd, %region_8.9_... | conditional | bytes 15728840 | solution.py:241
  7.0 8.9 %collective-permute-start.48 = (bf16[6,8,48,128]{3,2,1,0:T(8,128)(2,1)S(1)}, bf16[6,8,48,128]{3,2,1,0:T(8,128)(2,1)S(1)}, u32[]{:S(2)}, u32[]{:S(2)}) collective-permute-start(bf16[6,8,48,128]{3,2,1,0:T(8,128)(2,1)S(1)} %slice.157), channel_id=1, source_target_pairs={{64,0},{128,64},{192,128},{256,192},{320,256},{384,320},{448,384},... | collective-permute-start | bytes 1769480 | tf_op jit(solution)/shard_map/cond/branch_12_fun/ppermute | solution.py:24
  15.9 1.9 %collective-permute-start.49 = (bf16[6,8,48,128]{3,2,1,0:T(8,128)(2,1)S(1)}, bf16[6,8,48,128]{3,2,1,0:T(8,128)(2,1)S(1)}, u32[]{:S(2)}, u32[]{:S(2)}) collective-permute-start(bf16[6,8,48,128]{3,2,1,0:T(8,128)(2,1)S(1)} %slice.157), channel_id=1, source_target_pairs={{960,0},{0,64},{64,128},{128,192},{192,256},{256,320},{320,384},{3... | collective-permute-start | bytes 1769480 | tf_op jit(solution)/shard_map/cond/branch_12_fun/ppermute | solution.py:24
  17.8 3.6 %collective-permute-start.50 = (bf16[6,8,48,128]{3,2,1,0:T(8,128)(2,1)S(1)}, bf16[6,8,48,128]{3,2,1,0:T(8,128)(2,1)S(1)}, u32[]{:S(2)}, u32[]{:S(2)}) collective-permute-start(bf16[6,8,48,128]{3,2,1,0:T(8,128)(2,1)S(1)} %slice.157), channel_id=1, source_target_pairs={{128,0},{192,64},{256,128},{320,192},{384,256},{448,320},{512,384}... | collective-permute-start | bytes 1769480 | tf_op jit(solution)/shard_map/cond/branch_12_fun/ppermute | solution.py:24
  21.4 3.2 %collective-permute-start.51 = (bf16[6,8,48,128]{3,2,1,0:T(8,128)(2,1)S(1)}, bf16[6,8,48,128]{3,2,1,0:T(8,128)(2,1)S(1)}, u32[]{:S(2)}, u32[]{:S(2)}) collective-permute-start(bf16[6,8,48,128]{3,2,1,0:T(8,128)(2,1)S(1)} %slice.157), channel_id=1, source_target_pairs={{896,0},{960,64},{0,128},{64,192},{128,256},{192,320},{256,384},{3... | collective-permute-start | bytes 1769480 | tf_op jit(solution)/shard_map/cond/branch_12_fun/ppermute | solution.py:24
  24.6 15.5 %collective-permute-done.48 = bf16[6,8,48,128]{3,2,1,0:T(8,128)(2,1)S(1)} collective-permute-done((bf16[6,8,48,128]{3,2,1,0:T(8,128)(2,1)S(1)}, bf16[6,8,48,128]{3,2,1,0:T(8,128)(2,1)S(1)}, u32[]{:S(2)}, u32[]{:S(2)}) %collective-permute-start.48) | collective-permute-done | bytes 589856 | tf_op jit(solution)/shard_map/cond/branch_12_fun/ppermute | solution.py:24
  40.1 0.9 concatenate.179
  42.0 21.7 %collective-permute-done.50 = bf16[6,8,48,128]{3,2,1,0:T(8,128)(2,1)S(1)} collective-permute-done((bf16[6,8,48,128]{3,2,1,0:T(8,128)(2,1)S(1)}, bf16[6,8,48,128]{3,2,1,0:T(8,128)(2,1)S(1)}, u32[]{:S(2)}, u32[]{:S(2)}) %collective-permute-start.50) | collective-permute-done | bytes 589856 | tf_op jit(solution)/shard_map/cond/branch_12_fun/ppermute | solution.py:24
  66.5 1.9 %pad_add_fusion.count = s32[2]{0:T(128)} fusion(s32[1]{0:T(128)} %bitcast.3, s32[1]{0:T(128)} %bitcast.2), kind=kLoop, calls=%fused_computation.37 | loop fusion | flops 2 | bytes 16 | tf_op jit(solution)/shard_map/stack | solution.py:256
  68.3 6.4 %pairs.1 = f32[5,48,128]{2,1,0:T(8,128)} custom-call(s32[8]{0:T(128)} %copy-done.13, s32[2]{0:T(128)} %pad_add_fusion.count, f32[8,3]{1,0:T(8,128)} %broadcast_multiply_fusion.1.weight, bf16[8,8,48,128]{3,2,1,0:T(8,128)(2,1)} %bitcast.44, bf16[8,8,48,128]{3,2,1,0:T(8,128)(2,1)} %bitcast.47, bf16[7,8,48,128]{3,2,1,0:T(8,128)(2,1)} %get-tuple-element.26.up1, ...), custom_call_target="tpu_custom_call" | custom-call | tf_op jit(solution)/shard_map/pairs/pallas_call | solution.py:246
  76.6 1.9 %collective-permute-start.68 = (f32[69,4,128]{2,1,0:T(4,128)S(1)}, f32[69,4,128]{2,1,0:T(4,128)S(1)}, u32[]{:S(2)}, u32[]{:S(2)}) collective-permute-start(f32[69,4,128]{2,1,0:T(4,128)S(1)} %get-tuple-element.41), channel_id=1, source_target_pairs={{960,0},{0,64},{64,128},{128,192},{192,256},{256,320},{320,384},{3... | collective-permute-start | bytes 423944 | tf_op jit(solution)/shard_map/ppermute | solution.py:24
  78.5 7.6 %collective-permute-start.69 = (f32[69,4,128]{2,1,0:T(4,128)S(1)}, f32[69,4,128]{2,1,0:T(4,128)S(1)}, u32[]{:S(2)}, u32[]{:S(2)}) collective-permute-start(f32[69,4,128]{2,1,0:T(4,128)S(1)} %get-tuple-element.40), channel_id=1, source_target_pairs={{64,0},{128,64},{192,128},{256,192},{320,256},{384,320},{448,384},... | collective-permute-start | bytes 423944 | tf_op jit(solution)/shard_map/ppermute | solution.py:24
  86.1 1.9 %collective-permute-start.70 = (f32[24,4,128]{2,1,0:T(4,128)S(1)}, f32[24,4,128]{2,1,0:T(4,128)S(1)}, u32[]{:S(2)}, u32[]{:S(2)}) collective-permute-start(f32[24,4,128]{2,1,0:T(4,128)S(1)} %bitcast.53), channel_id=1, source_target_pairs={{896,0},{960,64},{0,128},{64,192},{128,256},{192,320},{256,384},{3... | collective-permute-start | bytes 147464 | tf_op jit(solution)/shard_map/ppermute | solution.py:24
  88.0 7.9 %collective-permute-start.71 = (f32[24,4,128]{2,1,0:T(4,128)S(1)}, f32[24,4,128]{2,1,0:T(4,128)S(1)}, u32[]{:S(2)}, u32[]{:S(2)}) collective-permute-start(f32[24,4,128]{2,1,0:T(4,128)S(1)} %bitcast.50), channel_id=1, source_target_pairs={{128,0},{192,64},{256,128},{320,192},{384,256},{448,320},{512,384}... | collective-permute-start | bytes 147464 | tf_op jit(solution)/shard_map/ppermute | solution.py:24
  95.9 1.9 %collective-permute-start.72 = (f32[12,4,128]{2,1,0:T(4,128)S(1)}, f32[12,4,128]{2,1,0:T(4,128)S(1)}, u32[]{:S(2)}, u32[]{:S(2)}) collective-permute-start(f32[12,4,128]{2,1,0:T(4,128)S(1)} %bitcast.68), channel_id=1, source_target_pairs={{832,0},{896,64},{960,128},{0,192},{64,256},{128,320},{192,384},{2... | collective-permute-start | bytes 73736 | tf_op jit(solution)/shard_map/ppermute | solution.py:24
  99.2 4.3 %collective-permute-done.72.r3 = f32[12,4,128]{2,1,0:T(4,128)S(1)} collective-permute-done((f32[12,4,128]{2,1,0:T(4,128)S(1)}, f32[12,4,128]{2,1,0:T(4,128)S(1)}, u32[]{:S(2)}, u32[]{:S(2)}) %collective-permute-start.72) | collective-permute-done | bytes 24608 | tf_op jit(solution)/shard_map/ppermute | solution.py:24
  103.5 2.0 %collective-permute-start.73 = (f32[12,4,128]{2,1,0:T(4,128)S(1)}, f32[12,4,128]{2,1,0:T(4,128)S(1)}, u32[]{:S(2)}, u32[]{:S(2)}) collective-permute-start(f32[12,4,128]{2,1,0:T(4,128)S(1)} %bitcast.67), channel_id=1, source_target_pairs={{192,0},{256,64},{320,128},{384,192},{448,256},{512,320},{576,384}... | collective-permute-start | bytes 73736 | tf_op jit(solution)/shard_map/ppermute | solution.py:24
  106.2 3.1 %collective-permute-done.73.m3 = f32[12,4,128]{2,1,0:T(4,128)S(1)} collective-permute-done((f32[12,4,128]{2,1,0:T(4,128)S(1)}, f32[12,4,128]{2,1,0:T(4,128)S(1)}, u32[]{:S(2)}, u32[]{:S(2)}) %collective-permute-start.73) | collective-permute-done | bytes 24608 | tf_op jit(solution)/shard_map/ppermute | solution.py:24
  110.0 2.0 %gather.8 = (f32[45,16,128]{2,1,0:T(8,128)}, f32[2,16,128]{2,1,0:T(8,128)}, f32[2,16,128]{2,1,0:T(8,128)}) custom-call(s32[2]{0:T(128)} %add_convert_fusion.inside, f32[60,4,128]{2,1,0:T(4,128)} %bitcast.48, f32[33,4,128]{2,1,0:T(4,128)} %pad_maximum_fusion.9.inputs, f32[69,4,128]{2,1,0:T(4,128)} %copy-done.1, f32[69,4,128]{2,1,0:T(4,128)} %copy-done.2, ...), custom_call_target="tpu_custom_call" | custom-call | tf_op jit(solution)/shard_map/gather/pallas_call | solution.py:281
  112.1 10.6 %collective-permute-start.74 = (f32[2,16,128]{2,1,0:T(8,128)}, f32[2,16,128]{2,1,0:T(8,128)S(1)}, u32[]{:S(2)}, u32[]{:S(2)}) collective-permute-start(f32[2,16,128]{2,1,0:T(8,128)} %get-tuple-element.31), channel_id=1, source_target_pairs={{1,0},{2,1},{3,2},{4,3},{5,4},{6,5},{7,6},{8,7},{9,8},{10,9},{11,1... | collective-permute-start | bytes 49160 | tf_op jit(solution)/shard_map/ppermute | solution.py:24
  122.7 3.9 %collective-permute-start.75 = (f32[2,16,128]{2,1,0:T(8,128)}, f32[2,16,128]{2,1,0:T(8,128)S(1)}, u32[]{:S(2)}, u32[]{:S(2)}) collective-permute-start(f32[2,16,128]{2,1,0:T(8,128)} %get-tuple-element.32), channel_id=1, source_target_pairs={{63,0},{0,1},{1,2},{2,3},{3,4},{4,5},{5,6},{6,7},{7,8},{8,9},{9,10... | collective-permute-start | bytes 49160 | tf_op jit(solution)/shard_map/ppermute | solution.py:24
  126.6 10.6 %collective-permute-done.75.from_west = f32[2,16,128]{2,1,0:T(8,128)S(1)} collective-permute-done((f32[2,16,128]{2,1,0:T(8,128)}, f32[2,16,128]{2,1,0:T(8,128)S(1)}, u32[]{:S(2)}, u32[]{:S(2)}) %collective-permute-start.75) | collective-permute-done | bytes 16416 | tf_op jit(solution)/shard_map/ppermute | solution.py:24
  137.8 3.1 %stencil.1 = f32[12,4,128]{2,1,0:T(4,128)} custom-call(f32[45,16,128]{2,1,0:T(8,128)} %get-tuple-element.30.field, f32[2,16,128]{2,1,0:T(8,128)} %copy-done.11, f32[2,16,128]{2,1,0:T(8,128)} %copy-done.12), custom_call_target="tpu_custom_call" | custom-call | tf_op jit(solution)/shard_map/stencil/pallas_call | solution.py:294
  141.0 1.9 %collective-permute-start.76 = (f32[12,4,128]{2,1,0:T(4,128)}, f32[12,4,128]{2,1,0:T(4,128)S(1)}, u32[]{:S(2)}, u32[]{:S(2)}) collective-permute-start(f32[12,4,128]{2,1,0:T(4,128)} %stencil.1), channel_id=1, source_target_pairs={{896,0},{960,64},{0,128},{64,192},{128,256},{192,320},{256,384},{3... | collective-permute-start | bytes 73736 | tf_op jit(solution)/shard_map/ppermute | solution.py:24
  142.9 3.7 %collective-permute-start.77 = (f32[12,4,128]{2,1,0:T(4,128)}, f32[12,4,128]{2,1,0:T(4,128)S(1)}, u32[]{:S(2)}, u32[]{:S(2)}) collective-permute-start(f32[12,4,128]{2,1,0:T(4,128)} %stencil.1), channel_id=1, source_target_pairs={{960,0},{0,64},{64,128},{128,192},{192,256},{256,320},{320,384},{3... | collective-permute-start | bytes 73736 | tf_op jit(solution)/shard_map/ppermute | solution.py:24
  146.6 7.3 %collective-permute-start.78 = (f32[12,4,128]{2,1,0:T(4,128)}, f32[12,4,128]{2,1,0:T(4,128)S(1)}, u32[]{:S(2)}, u32[]{:S(2)}) collective-permute-start(f32[12,4,128]{2,1,0:T(4,128)} %stencil.1), channel_id=1, source_target_pairs={{64,0},{128,64},{192,128},{256,192},{320,256},{384,320},{448,384},... | collective-permute-start | bytes 73736 | tf_op jit(solution)/shard_map/ppermute | solution.py:24
  153.9 3.1 %collective-permute-start.79 = (f32[12,4,128]{2,1,0:T(4,128)}, f32[12,4,128]{2,1,0:T(4,128)S(1)}, u32[]{:S(2)}, u32[]{:S(2)}) collective-permute-start(f32[12,4,128]{2,1,0:T(4,128)} %stencil.1), channel_id=1, source_target_pairs={{128,0},{192,64},{256,128},{320,192},{384,256},{448,320},{512,384}... | collective-permute-start | bytes 73736 | tf_op jit(solution)/shard_map/ppermute | solution.py:24
  158.6 12.8 %all-to-all-start = ((f32[64,1,48]{2,1,0:T(1,128)}), f32[64,1,48]{2,1,0:T(1,128)S(1)}, u32[]{:S(2)}, u32[]{:S(2)}) async-start(f32[64,1,48]{2,1,0:T(1,128)} %broadcast_in_dim.65), calls=%async_computation | async-start | bytes 65536 | tf_op jit(solution)/shard_map/all_to_all | solution.py:308
  172.9 7.3 %mixed.1 = f32[8,8,48,128]{3,2,1,0:T(8,128)} custom-call(s32[8]{0:T(128)} %copy-done.15, f32[8,3]{1,0:T(8,128)} %copy-done.7, f32[5,48,128]{2,1,0:T(8,128)} %broadcast_multiply_fusion.sens, bf16[8,8,48,128]{3,2,1,0:T(8,128)(2,1)} %bitcast.45, bf16[7,8,48,128]{3,2,1,0:T(8,128)(2,1)} %get-tuple-element.26.up1, ...), custom_call_target="tpu_custom_call" | custom-call | tf_op jit(solution)/shard_map/mixed/pallas_call | solution.py:314
  180.2 4.5 %all-to-all-done = f32[64,1,48]{2,1,0:T(1,128)S(1)} async-done(((f32[64,1,48]{2,1,0:T(1,128)}), f32[64,1,48]{2,1,0:T(1,128)S(1)}, u32[]{:S(2)}, u32[]{:S(2)}) %all-to-all-start) | async-done | bytes 12320 | tf_op jit(solution)/shard_map/all_to_all | solution.py:308
  (81 shorter events, 14.3 us)
Async XLA Ops:
  2.9 4.0 %copy-start.15 = (s32[8]{0:T(128)}, s32[8]{0:T(128)S(1)}, u32[]{:S(2)}) copy-start(s32[8]{0:T(128)S(1)} %convert_reduce_fusion.rank) | copy-start | bytes 100
  3.0 3.9 %copy-start.13 = (s32[8]{0:T(128)}, s32[8]{0:T(128)S(1)}, u32[]{:S(2)}) copy-start(s32[8]{0:T(128)S(1)} %select_reduce_fusion.1.order) | copy-start | bytes 100
  7.0 33.2 %collective-permute-start.48 = (bf16[6,8,48,128]{3,2,1,0:T(8,128)(2,1)S(1)}, bf16[6,8,48,128]{3,2,1,0:T(8,128)(2,1)S(1)}, u32[]{:S(2)}, u32[]{:S(2)}) collective-permute-start(bf16[6,8,48,128]{3,2,1,0:T(8,128)(2,1)S(1)} %slice.157), channel_id=1, source_target_pairs={{64,0},{128,64},{192,128},{256,192},{320,256},{384,320},{448,384},... | collective-permute-start | bytes 1769480 | tf_op jit(solution)/shard_map/cond/branch_12_fun/ppermute | solution.py:24
  15.9 25.2 %collective-permute-start.49 = (bf16[6,8,48,128]{3,2,1,0:T(8,128)(2,1)S(1)}, bf16[6,8,48,128]{3,2,1,0:T(8,128)(2,1)S(1)}, u32[]{:S(2)}, u32[]{:S(2)}) collective-permute-start(bf16[6,8,48,128]{3,2,1,0:T(8,128)(2,1)S(1)} %slice.157), channel_id=1, source_target_pairs={{960,0},{0,64},{64,128},{128,192},{192,256},{256,320},{320,384},{3... | collective-permute-start | bytes 1769480 | tf_op jit(solution)/shard_map/cond/branch_12_fun/ppermute | solution.py:24
  17.8 45.9 %collective-permute-start.50 = (bf16[6,8,48,128]{3,2,1,0:T(8,128)(2,1)S(1)}, bf16[6,8,48,128]{3,2,1,0:T(8,128)(2,1)S(1)}, u32[]{:S(2)}, u32[]{:S(2)}) collective-permute-start(bf16[6,8,48,128]{3,2,1,0:T(8,128)(2,1)S(1)} %slice.157), channel_id=1, source_target_pairs={{128,0},{192,64},{256,128},{320,192},{384,256},{448,320},{512,384}... | collective-permute-start | bytes 1769480 | tf_op jit(solution)/shard_map/cond/branch_12_fun/ppermute | solution.py:24
  21.4 43.2 %collective-permute-start.51 = (bf16[6,8,48,128]{3,2,1,0:T(8,128)(2,1)S(1)}, bf16[6,8,48,128]{3,2,1,0:T(8,128)(2,1)S(1)}, u32[]{:S(2)}, u32[]{:S(2)}) collective-permute-start(bf16[6,8,48,128]{3,2,1,0:T(8,128)(2,1)S(1)} %slice.157), channel_id=1, source_target_pairs={{896,0},{960,64},{0,128},{64,192},{128,256},{192,320},{256,384},{3... | collective-permute-start | bytes 1769480 | tf_op jit(solution)/shard_map/cond/branch_12_fun/ppermute | solution.py:24
  65.6 9.1 %copy-start.7 = (f32[8,3]{1,0:T(8,128)}, f32[8,3]{1,0:T(8,128)S(1)}, u32[]{:S(2)}) copy-start(f32[8,3]{1,0:T(8,128)S(1)} %fusion.weight) | copy-start | bytes 292
  68.3 8.0 %copy-start.14 = (s32[4,128]{1,0:T(4,128)S(1)}, s32[4,128]{1,0:T(4,128)}, u32[]{:S(2)}) copy-start(s32[4,128]{1,0:T(4,128)} %param.30) | copy-start | bytes 6148
  68.3 8.0 %copy-start.3 = (f32[3,4,4,128]{3,2,1,0:T(4,128)S(1)}, f32[3,4,4,128]{3,2,1,0:T(4,128)}, u32[]{:S(2)}) copy-start(f32[3,4,4,128]{3,2,1,0:T(4,128)} %param.28) | copy-start | bytes 73732
  68.3 8.0 %copy-start.10 = (f32[3,4,4]{2,1,0:T(4,128)S(1)}, f32[3,4,4]{2,1,0:T(4,128)}, u32[]{:S(2)}) copy-start(f32[3,4,4]{2,1,0:T(4,128)} %param.27) | copy-start | bytes 580
  68.3 8.2 %copy-start = (f32[2,3,4,4,128]{4,3,2,1,0:T(4,128)S(1)}, f32[2,3,4,4,128]{4,3,2,1,0:T(4,128)}, u32[]{:S(2)}) copy-start(f32[2,3,4,4,128]{4,3,2,1,0:T(4,128)} %param.31) | copy-start | bytes 147460
  68.3 8.2 %copy-start.4 = (f32[2,4,4,128]{3,2,1,0:T(4,128)S(1)}, f32[2,4,4,128]{3,2,1,0:T(4,128)}, u32[]{:S(2)}) copy-start(f32[2,4,4,128]{3,2,1,0:T(4,128)} %param.29) | copy-start | bytes 49156
  76.6 32.7 %collective-permute-start.68 = (f32[69,4,128]{2,1,0:T(4,128)S(1)}, f32[69,4,128]{2,1,0:T(4,128)S(1)}, u32[]{:S(2)}, u32[]{:S(2)}) collective-permute-start(f32[69,4,128]{2,1,0:T(4,128)S(1)} %get-tuple-element.41), channel_id=1, source_target_pairs={{960,0},{0,64},{64,128},{128,192},{192,256},{256,320},{320,384},{3... | collective-permute-start | bytes 423944 | tf_op jit(solution)/shard_map/ppermute | solution.py:24
  78.5 30.8 %collective-permute-start.69 = (f32[69,4,128]{2,1,0:T(4,128)S(1)}, f32[69,4,128]{2,1,0:T(4,128)S(1)}, u32[]{:S(2)}, u32[]{:S(2)}) collective-permute-start(f32[69,4,128]{2,1,0:T(4,128)S(1)} %get-tuple-element.40), channel_id=1, source_target_pairs={{64,0},{128,64},{192,128},{256,192},{320,256},{384,320},{448,384},... | collective-permute-start | bytes 423944 | tf_op jit(solution)/shard_map/ppermute | solution.py:24
  86.1 23.2 %collective-permute-start.70 = (f32[24,4,128]{2,1,0:T(4,128)S(1)}, f32[24,4,128]{2,1,0:T(4,128)S(1)}, u32[]{:S(2)}, u32[]{:S(2)}) collective-permute-start(f32[24,4,128]{2,1,0:T(4,128)S(1)} %bitcast.53), channel_id=1, source_target_pairs={{896,0},{960,64},{0,128},{64,192},{128,256},{192,320},{256,384},{3... | collective-permute-start | bytes 147464 | tf_op jit(solution)/shard_map/ppermute | solution.py:24
  88.0 21.2 %collective-permute-start.71 = (f32[24,4,128]{2,1,0:T(4,128)S(1)}, f32[24,4,128]{2,1,0:T(4,128)S(1)}, u32[]{:S(2)}, u32[]{:S(2)}) collective-permute-start(f32[24,4,128]{2,1,0:T(4,128)S(1)} %bitcast.50), channel_id=1, source_target_pairs={{128,0},{192,64},{256,128},{320,192},{384,256},{448,320},{512,384}... | collective-permute-start | bytes 147464 | tf_op jit(solution)/shard_map/ppermute | solution.py:24
  95.9 7.6 %collective-permute-start.72 = (f32[12,4,128]{2,1,0:T(4,128)S(1)}, f32[12,4,128]{2,1,0:T(4,128)S(1)}, u32[]{:S(2)}, u32[]{:S(2)}) collective-permute-start(f32[12,4,128]{2,1,0:T(4,128)S(1)} %bitcast.68), channel_id=1, source_target_pairs={{832,0},{896,64},{960,128},{0,192},{64,256},{128,320},{192,384},{2... | collective-permute-start | bytes 73736 | tf_op jit(solution)/shard_map/ppermute | solution.py:24
  103.5 5.8 %copy-start.8 = (f32[12,4,128]{2,1,0:T(4,128)}, f32[12,4,128]{2,1,0:T(4,128)S(1)}, u32[]{:S(2)}) copy-start(f32[12,4,128]{2,1,0:T(4,128)S(1)} %collective-permute-done.72.r3) | copy-start | bytes 73732
  103.5 5.8 %collective-permute-start.73 = (f32[12,4,128]{2,1,0:T(4,128)S(1)}, f32[12,4,128]{2,1,0:T(4,128)S(1)}, u32[]{:S(2)}, u32[]{:S(2)}) collective-permute-start(f32[12,4,128]{2,1,0:T(4,128)S(1)} %bitcast.67), channel_id=1, source_target_pairs={{192,0},{256,64},{320,128},{384,192},{448,256},{512,320},{576,384}... | collective-permute-start | bytes 73736 | tf_op jit(solution)/shard_map/ppermute | solution.py:24
  109.3 0.6 copy-start.9
  109.3 0.6 copy-start.5
  109.3 0.6 copy-start.6
  109.3 0.7 copy-start.1
  109.3 0.7 copy-start.2
  112.1 14.5 %collective-permute-start.74 = (f32[2,16,128]{2,1,0:T(8,128)}, f32[2,16,128]{2,1,0:T(8,128)S(1)}, u32[]{:S(2)}, u32[]{:S(2)}) collective-permute-start(f32[2,16,128]{2,1,0:T(8,128)} %get-tuple-element.31), channel_id=1, source_target_pairs={{1,0},{2,1},{3,2},{4,3},{5,4},{6,5},{7,6},{8,7},{9,8},{10,9},{11,1... | collective-permute-start | bytes 49160 | tf_op jit(solution)/shard_map/ppermute | solution.py:24
  122.7 14.5 %collective-permute-start.75 = (f32[2,16,128]{2,1,0:T(8,128)}, f32[2,16,128]{2,1,0:T(8,128)S(1)}, u32[]{:S(2)}, u32[]{:S(2)}) collective-permute-start(f32[2,16,128]{2,1,0:T(8,128)} %get-tuple-element.32), channel_id=1, source_target_pairs={{63,0},{0,1},{1,2},{2,3},{3,4},{4,5},{5,6},{6,7},{7,8},{8,9},{9,10... | collective-permute-start | bytes 49160 | tf_op jit(solution)/shard_map/ppermute | solution.py:24
  126.6 10.6 %copy-start.11 = (f32[2,16,128]{2,1,0:T(8,128)}, f32[2,16,128]{2,1,0:T(8,128)S(1)}, u32[]{:S(2)}) copy-start(f32[2,16,128]{2,1,0:T(8,128)S(1)} %collective-permute-done.74.from_east) | copy-start | bytes 49156
  141.0 30.5 %collective-permute-start.76 = (f32[12,4,128]{2,1,0:T(4,128)}, f32[12,4,128]{2,1,0:T(4,128)S(1)}, u32[]{:S(2)}, u32[]{:S(2)}) collective-permute-start(f32[12,4,128]{2,1,0:T(4,128)} %stencil.1), channel_id=1, source_target_pairs={{896,0},{960,64},{0,128},{64,192},{128,256},{192,320},{256,384},{3... | collective-permute-start | bytes 73736 | tf_op jit(solution)/shard_map/ppermute | solution.py:24
  142.9 28.6 %collective-permute-start.77 = (f32[12,4,128]{2,1,0:T(4,128)}, f32[12,4,128]{2,1,0:T(4,128)S(1)}, u32[]{:S(2)}, u32[]{:S(2)}) collective-permute-start(f32[12,4,128]{2,1,0:T(4,128)} %stencil.1), channel_id=1, source_target_pairs={{960,0},{0,64},{64,128},{128,192},{192,256},{256,320},{320,384},{3... | collective-permute-start | bytes 73736 | tf_op jit(solution)/shard_map/ppermute | solution.py:24
  146.6 25.6 %collective-permute-start.78 = (f32[12,4,128]{2,1,0:T(4,128)}, f32[12,4,128]{2,1,0:T(4,128)S(1)}, u32[]{:S(2)}, u32[]{:S(2)}) collective-permute-start(f32[12,4,128]{2,1,0:T(4,128)} %stencil.1), channel_id=1, source_target_pairs={{64,0},{128,64},{192,128},{256,192},{320,256},{384,320},{448,384},... | collective-permute-start | bytes 73736 | tf_op jit(solution)/shard_map/ppermute | solution.py:24
  153.9 18.3 %collective-permute-start.79 = (f32[12,4,128]{2,1,0:T(4,128)}, f32[12,4,128]{2,1,0:T(4,128)S(1)}, u32[]{:S(2)}, u32[]{:S(2)}) collective-permute-start(f32[12,4,128]{2,1,0:T(4,128)} %stencil.1), channel_id=1, source_target_pairs={{128,0},{192,64},{256,128},{320,192},{384,256},{448,320},{512,384}... | collective-permute-start | bytes 73736 | tf_op jit(solution)/shard_map/ppermute | solution.py:24
  158.6 26.1 %all-to-all-start = ((f32[64,1,48]{2,1,0:T(1,128)}), f32[64,1,48]{2,1,0:T(1,128)S(1)}, u32[]{:S(2)}, u32[]{:S(2)}) async-start(f32[64,1,48]{2,1,0:T(1,128)} %broadcast_in_dim.65), calls=%async_computation | async-start | bytes 65536 | tf_op jit(solution)/shard_map/all_to_all | solution.py:308
  (1 other events, 0.6 us)
